TPU v7x, 32 devices: a whole 2x2x4 slice. The times are simulated.
32 devices in a mesh: row: 4 (over z), col: 8 (over y, x, core).
Axes of the slice: x: 2, y: 2, z: 4, core: 2. Of those that a mesh axis runs over, the one named last changes fastest.
Arguments:
- out_grads: bfloat16 [8, 48, 28672], P('col', None, 'row'), may hold values from -6 to 6
- acts: bfloat16 [8, 48, 8192], P('row', None, 'col'), may hold values from -6 to 6
- rot_out: bfloat16 [28672, 28672], P('row', 'col'), may hold values from -0.03125 to 0.03125
- rot_in: bfloat16 [8192, 8192], P('col', 'row'), may hold values from -0.0625 to 0.0625
- queries: bfloat16 [2, 28672, 8192], P(None, 'col', 'row'), may hold values from -0.00036621094 to 0.00036621094
- token_sequence: int32 [256], replicated, may hold values from 0 to 7, never falling along the last dimension, each value on 1 to 48 neighbouring positions
Outputs:
- scores: float32 [256, 2], P(('row', 'col'))
Inputs may be any that keep to these rules, and one draw needn't show every extreme that they name: `token_sequence`: values never fall along the tokens; every sequence 0 to 7 has 1 to 48 tokens, some sequence exactly 48; the k-th token of a sequence (from 0) sits in its slot k of out_grads and acts.
All inputs are finite; a program needn't handle non-finite values.
Results may differ from a plain program's by a relative error of at most 0.0041.
Values may be sent and summed in bfloat16 or wider, within the bound.
No kernel may reach another device: no remote copies, remote signals or barrier semaphores. Data moves between devices by JAX's collectives and lax.ppermute only.
A program may use at most 128 MiB of HBM per device.

v0:
```python
import jax
import jax.numpy as jnp
from jax import lax
from jax.sharding import PartitionSpec as P


def token_places(token_sequence, seq_count, slot_count):
    token_count = token_sequence.shape[0]
    labels = jnp.arange(seq_count, dtype=jnp.int32)
    before = (token_sequence[:, None] < labels[None, :]).astype(jnp.int32)
    starts = jnp.sum(before, axis=0)
    member = (token_sequence[:, None] == labels[None, :]).astype(jnp.int32)
    own_start = jnp.sum(member * starts[None, :], axis=1)
    position = jnp.arange(token_count, dtype=jnp.int32) - own_start
    return token_sequence * slot_count + position


def local(out_grads, acts, rot_out, rot_in, queries, token_sequence):
    slot_count = out_grads.shape[1]
    seq_count = out_grads.shape[0] * lax.axis_size("col")
    flat_index = token_places(token_sequence, seq_count, slot_count)
    act_slots = lax.all_gather(acts, "row", axis=0, tiled=True)
    act_rows = jnp.take(
        act_slots.reshape(seq_count * slot_count, act_slots.shape[2]), flat_index, axis=0
    )
    grad_slots = lax.all_gather(out_grads, "col", axis=0, tiled=True)
    grad_rows = jnp.take(
        grad_slots.reshape(seq_count * slot_count, grad_slots.shape[2]), flat_index, axis=0
    )
    picked = grad_rows
    rot_grads = lax.psum(
        jnp.dot(picked, rot_out, preferred_element_type=jnp.float32), "row"
    ).astype(jnp.bfloat16)
    picked = act_rows
    rot_acts = lax.psum(jnp.dot(picked, rot_in, preferred_element_type=jnp.float32), "col").astype(
        jnp.bfloat16
    )
    projected = jnp.einsum("tj,qij->tqi", rot_acts, queries, preferred_element_type=jnp.float32)
    score_terms = jnp.sum(projected * rot_grads[:, None, :], axis=2)
    return lax.psum_scatter(score_terms, ("row", "col"), scatter_dimension=0, tiled=True)


def solution(mesh):
    placed = (
        P("col", None, "row"),
        P("row", None, "col"),
        P("row", "col"),
        P("col", "row"),
        P(None, "col", "row"),
        P(),
    )
    return jax.shard_map(
        local, mesh=mesh, in_specs=placed, out_specs=P(("row", "col"), None), check_vma=False
    )
```

profile of v0, /device:TPU:0, one launch (start us, length us, event | category | flops | bytes accessed | tf_op | source)
XLA Modules:
  0.0 327.6 jit_solution(2703172752374178728)
XLA Ops:
  6.5 0.0 all-gather.2.cloned.1.call-start
  6.5 0.7 all-gather.2.cloned.1.call-update
  7.3 0.8 convert_reduce_fusion
  8.1 0.8 select_reduce_fusion
  8.8 0.7 compare_and_fusion
  9.5 21.5 %all_gather.6 = bf16[8,48,1024]{2,1,0:T(8,128)(2,1)S(1)} all-gather(bf16[2,48,1024]{2,1,0:T(8,128)(2,1)} %param.7), channel_id=1, replica_groups=mesh['row'=4,'col'=8] {'row'}, dimensions={0}, use_global_device_ids=true | all-gather | bytes 983040 | tf_op jit(solution)/shard_map/all_gather | solution.py:22
  31.0 1.2 gather_fusion
  32.2 3.5 %fusion.6 = f32[256,2048]{1,0:T(8,128)S(1)} fusion(bf16[1024,2048]{1,0:T(8,128)(2,1)} %param.9, bf16[256,1024]{1,0:T(8,128)(2,1)S(1)} %gather_fusion, pred[256]{0:T(512)(128)(4,1)S(1)} %get-tuple-element.5), kind=kOutput, calls=%fused_computation.10 | convolution fusion | flops 1074003968 | bytes 6816000 | tf_op jit(solution)/shard_map/dot_general | solution.py:35
  35.7 65.4 %all-reduce.4 = bf16[256,2048]{1,0:T(8,128)(2,1)S(1)} all-reduce(f32[256,2048]{1,0:T(8,128)S(1)} %fusion.6), channel_id=1, replica_groups=mesh['row'=4,'col'=8] {'col'}, use_global_device_ids=true, to_apply=%region_2.3 | all-reduce | flops 524288 | bytes 3145728 | tf_op jit(solution)/shard_map/psum | solution.py:35
  101.1 0.0 all-gather.2.cloned.1.call-done
  101.1 11.3 %gather_fusion.1 = bf16[256,7168]{1,0:T(8,128)(2,1)} fusion(bf16[384,7168]{1,0:T(8,128)(2,1)} %bitcast.10, s32[1024]{0:T(1024)S(1)} %pad_clamp_fusion), kind=kCustom, calls=%fused_computation.1 | custom fusion | bytes 7341056 | tf_op jit(solution)/shard_map/jit(_take)/gather | solution.py:27
  112.5 24.3 %fusion = f32[256,3584]{1,0:T(8,128)} fusion(bf16[7168,3584]{1,0:T(8,128)(2,1)} %param.8, bf16[256,7168]{1,0:T(8,128)(2,1)} %gather_fusion.1, pred[256]{0:T(512)(128)(4,1)S(1)} %get-tuple-element.5), kind=kOutput, calls=%fused_computation.3 | convolution fusion | flops 13155172352 | bytes 58720512 | tf_op jit(solution)/shard_map/dot_general | solution.py:32
  136.8 127.4 %all-reduce.3 = bf16[256,3584]{1,0:T(8,128)(2,1)S(1)} all-reduce(f32[256,3584]{1,0:T(8,128)} %fusion), channel_id=1, replica_groups=mesh['row'=4,'col'=8] {'row'}, use_global_device_ids=true, to_apply=%region_3.4 | all-reduce | flops 917504 | bytes 5505024 | tf_op jit(solution)/shard_map/psum | solution.py:31
  264.2 2.2 convert_element_type.25
  266.4 14.7 %multiply_reduce_fusion = f32[256,2]{0,1:T(2,128)S(1)} fusion(bf16[2,3584,2048]{2,1,0:T(8,128)(2,1)} %param.10, f32[256,3584]{1,0:T(8,128)} %convert_element_type.25, bf16[256,2048]{1,0:T(8,128)(2,1)S(1)} %all-reduce.4), kind=kOutput, calls=%fused_computation.2 | convolution fusion | flops 7519862272 | bytes 34080768 | tf_op jit(solution)/shard_map/tj,qij->tqi/dot_general | solution.py:38
  281.1 39.0 %all-reduce = f32[256,2]{0,1:T(2,128)S(1)} all-reduce(f32[256,2]{0,1:T(2,128)S(1)} %multiply_reduce_fusion), channel_id=2, replica_groups=mesh['row'=4,'col'=8] {'row','col'}, use_global_device_ids=true, to_apply=%region_5.6.clone | all-reduce | flops 512 | bytes 4096
  320.1 0.6 constant_dynamic-slice_fusion
  (1 shorter events, 0.0 us)
Async XLA Ops:
  6.5 94.6 %all-gather.2.cloned.1.call-start = ((), (), s32[]{:S(2)}) async-start(), calls=%async_computation | async-start | bytes 6193152 | tf_op jit(solution)/shard_map/all_gather | solution.py:26
Sparse Core Ops, SparseCore 0:
  9.2 56.0 all-gather.1
where the time goes:
time: 328 us
  blocking collectives  253 us (77%)
  matrix products  42.5 us (13%)
  between operations  13.5 us (4%)
  local copies, waits for them, and re-layouts  13.1 us (4%)
  other arithmetic  4.48 us (1%)
    psum x1, blocking collectives, local(): lax.psum(jnp.dot(picked, rot_out, preferred_element_type=jnp.float32), 'r...  127 us
    psum x1, blocking collectives, local(): lax.psum(jnp.dot(picked, rot_in, preferred_element_type=jnp.float32), 'col')  65.4 us
    unnamed x1, blocking collectives  39 us
    dot_general x1, matrix products, local(): jnp.dot(picked, rot_out, preferred_element_type=jnp.float32)  24.3 us
    all_gather x1, blocking collectives, local(): act_slots = lax.all_gather(acts, 'row', axis=0, tiled=True)  21.5 us
    dot_general x1, matrix products, local(): jnp.einsum('tj,qij->tqi', rot_acts, queries, preferred_element_type=jnp.f...  14.7 us
    gather x1, local copies, waits for them, and re-layouts, local(): jnp.take(grad_slots.reshape(seq_count * slot_count, grad_slots.shape[2]),...  11.3 us
  transfers between devices with their start and end apart: 1, of which 0 were waited for; matrix products, arithmetic and copies ran while one was open for 2% of the time, Pallas kernels for 0%

commit v1 on v0

v1 whole, which is shorter than its diff:
```python
import jax
import jax.numpy as jnp
from jax import lax
from jax.experimental import pallas as pl
from jax.experimental.pallas import tpu as pltpu
from jax.sharding import PartitionSpec as P

F32 = jnp.float32
BF16 = jnp.bfloat16
LANES = 128
WIDE = 512
CHUNKS = 4


def block_of(size, limit):
    best = LANES
    for width in range(LANES, min(size, limit) + 1, LANES):
        if size % width == 0:
            best = width
    return best


def limit(need):
    return pltpu.CompilerParams(vmem_limit_bytes=max(need + (6 << 20), 24 << 20))


class Column:
    def __init__(self, axis):
        self.axis = axis
        self.count = lax.axis_size(axis)
        self.stages = max(self.count.bit_length() - 2, 0)
        self.index = lax.axis_index(axis)

    def near(self, value):
        return lax.ppermute(value, self.axis, [(i, i ^ 1) for i in range(self.count)])

    def far(self, value, stage):
        def partner(i):
            return i ^ (2 << (stage if i % 2 == 0 else self.stages - 1 - stage))

        return lax.ppermute(value, self.axis, [(i, partner(i)) for i in range(self.count)])

    def reverse(self, value):
        out = jnp.zeros_like(value)
        for b in range(self.stages):
            out = out | (((value >> b) & 1) << (self.stages - 1 - b))
        return out

    def arrival(self, source):
        apart = source ^ self.index
        links = apart >> 1
        stage_bits = jnp.where((source & 1) == 0, links, self.reverse(links))
        return ((apart & 1) << self.stages) + stage_bits

    def place(self, target):
        apart = target ^ self.index
        links = apart >> 1
        stage_bits = jnp.where((target & 1) == 0, self.reverse(links), links)
        return ((apart & 1) << self.stages) + stage_bits

    def gather(self, own):
        have = [own]
        far = []
        for s in range(self.stages):
            far.append([self.far(own, s)])
        for s in range(self.stages):
            far[s] = far[s] + [self.far(block, s) for block in have[1:]]
            have = have + far[s]
        out = []
        for block in have:
            out.append(self.near(block))
        return have + out

    def reduce(self, low, high):
        part = low + self.near(high)
        for s in range(self.stages):
            half = part.shape[0] // 2
            part = part[:half] + self.far(part[half:], s)
        return part

    def spread(self, part):
        for s in reversed(range(self.stages)):
            part = jnp.concatenate([part, self.far(part, s)], axis=0)
        return jnp.concatenate([part, self.near(part)], axis=0)


def token_slots(token_sequence, seq_count):
    labels = jnp.arange(seq_count, dtype=jnp.int32)
    before = (token_sequence[:, None] < labels[None, :]).astype(jnp.int32)
    starts = jnp.sum(before, axis=0)
    member = (token_sequence[:, None] == labels[None, :]).astype(jnp.int32)
    own_start = jnp.sum(member * starts[None, :], axis=1)
    return jnp.arange(token_sequence.shape[0], dtype=jnp.int32) - own_start


def one_hot(index, width):
    return (index[:, None] == jnp.arange(width, dtype=jnp.int32)[None, :]).astype(BF16)


def fetch(sources, target, sems):
    copies, at = [], 0
    for k, source in enumerate(sources):
        rows = source.shape[0]
        copies.append(pltpu.make_async_copy(source, target.at[pl.ds(at, rows)], sems.at[k]))
        copies[-1].start()
        at += rows
    return copies


def in_hbm(values):
    return [pltpu.with_memory_space_constraint(v, pltpu.HBM) for v in values]


HBM = pl.BlockSpec(memory_space=pltpu.HBM)
VMEM = pl.BlockSpec(memory_space=pltpu.VMEM)


def pack_rows(onehot, blocks):
    tokens, slots_all = onehot.shape
    features = blocks[0].shape[1]
    width = block_of(features, 1792)
    parts = features // width

    def kernel(onehot_ref, *refs):
        sources, (out_ref, rows_ref, sems) = refs[:-3], refs[-3:]
        copies = []

        def start(p):
            columns = pl.ds(p * width, width)
            copies.append(
                fetch([r.at[:, columns] for r in sources], rows_ref.at[:, columns], sems.at[p])
            )

        start(0)
        for p in range(parts):
            if p + 1 < parts:
                start(p + 1)
            for copy in copies[p]:
                copy.wait()
            columns = pl.ds(p * width, width)
            out_ref[:, columns] = jnp.dot(
                onehot_ref[...], rows_ref[:, columns], preferred_element_type=F32
            ).astype(BF16)

    return pl.pallas_call(
        kernel,
        in_specs=[VMEM] + [HBM] * len(blocks),
        out_specs=VMEM,
        out_shape=jax.ShapeDtypeStruct((tokens, features), BF16),
        scratch_shapes=[
            pltpu.VMEM((slots_all, features), BF16),
            pltpu.SemaphoreType.DMA((parts, len(blocks))),
        ],
        compiler_params=limit(2 * (tokens * slots_all + (slots_all + 2 * tokens) * features)),
        cost_estimate=pl.CostEstimate(
            flops=2 * tokens * slots_all * features,
            bytes_accessed=2 * features * (tokens + slots_all),
            transcendentals=0,
        ),
        name="pack_grads",
    )(onehot, *in_hbm(blocks))


def rotate_grads(rows, basis, start, width):
    tokens, depth = rows.shape
    unit = block_of(width, WIDE)
    deep = block_of(depth, 1792)
    pieces = [(i, k) for i in range(width // unit) for k in range(depth // deep)]
    ahead = min(4, len(pieces))

    def kernel(rows_ref, basis_ref, sum_ref, sent_ref, held_ref, sems):
        def copy(n):
            i, k = pieces[n]
            return pltpu.make_async_copy(
                basis_ref.at[pl.ds(k * deep, deep), pl.ds(start + i * unit, unit)],
                held_ref.at[n % (ahead + 1)],
                sems.at[n % (ahead + 1)],
            )

        for n in range(ahead):
            copy(n).start()
        for n, (i, k) in enumerate(pieces):
            if n + ahead < len(pieces):
                copy(n + ahead).start()
            copy(n).wait()
            part = jnp.dot(
                rows_ref[:, pl.ds(k * deep, deep)],
                held_ref[n % (ahead + 1)],
                preferred_element_type=F32,
            )
            columns = pl.ds(i * unit, unit)
            if k > 0:
                part = sum_ref[:, columns] + part
            sum_ref[:, columns] = part
            if k == depth // deep - 1:
                sent_ref[:, columns] = part.astype(BF16)

    return pl.pallas_call(
        kernel,
        in_specs=[VMEM, HBM],
        out_specs=[VMEM, VMEM],
        out_shape=[
            jax.ShapeDtypeStruct((tokens, width), F32),
            jax.ShapeDtypeStruct((tokens, width), BF16),
        ],
        scratch_shapes=[
            pltpu.VMEM((ahead + 1, deep, unit), BF16),
            pltpu.SemaphoreType.DMA((ahead + 1,)),
        ],
        compiler_params=limit(2 * (ahead + 1) * deep * unit + 2 * tokens * (depth + 4 * width)),
        cost_estimate=pl.CostEstimate(
            flops=2 * tokens * depth * width,
            bytes_accessed=2 * depth * (width + tokens) + 6 * tokens * width,
            transcendentals=0,
        ),
        name="rotate_grads",
    )(rows, *in_hbm([basis]))


def rotate_acts(onehot, blocks, basis):
    tokens, slots_all = onehot.shape
    depth, width = basis.shape
    unit = block_of(width, WIDE)
    half = tokens // 2

    def kernel(onehot_ref, *refs):
        sources = refs[:-5]
        basis_ref, low_ref, high_ref, held_ref, sems = refs[-5:]
        copies = []
        for k, at in enumerate(range(0, width, unit)):
            columns = pl.ds(at, unit)
            copies.append(
                pltpu.make_async_copy(basis_ref.at[:, columns], held_ref.at[:, columns], sems.at[k])
            )
            copies[k].start()
        slots = jnp.concatenate([r[...] for r in sources], axis=0)
        rows = jnp.dot(onehot_ref[...], slots, preferred_element_type=F32).astype(BF16)
        for k, at in enumerate(range(0, width, unit)):
            columns = pl.ds(at, unit)
            copies[k].wait()
            part = jnp.dot(rows, held_ref[:, columns], preferred_element_type=F32)
            low_ref[:, columns] = part[:half]
            high_ref[:, columns] = part[half:]

    shape = jax.ShapeDtypeStruct((half, width), F32)
    return pl.pallas_call(
        kernel,
        in_specs=[VMEM] * (len(blocks) + 1) + [HBM],
        out_specs=[VMEM, VMEM],
        out_shape=[shape, shape],
        scratch_shapes=[
            pltpu.VMEM((depth, width), BF16),
            pltpu.SemaphoreType.DMA((width // unit,)),
        ],
        compiler_params=limit(
            2 * (tokens * slots_all + (2 * slots_all + width + 3 * tokens) * depth) + 6 * tokens * width
        ),
        cost_estimate=pl.CostEstimate(
            flops=2 * tokens * depth * (width + slots_all),
            bytes_accessed=2 * depth * (width + slots_all) + 4 * tokens * width,
            transcendentals=0,
        ),
        name="rotate_acts",
    )(onehot, *blocks, *in_hbm([basis]))


def project(rot_acts, queries, start, width):
    count, _, depth = queries.shape
    tokens = rot_acts.shape[0]
    unit = block_of(width, WIDE)
    pieces = [(q, i) for q in range(count) for i in range(width // unit)]
    ahead = min(3, len(pieces))

    def kernel(acts_ref, queries_ref, out_ref, held_ref, sems):
        def copy(n):
            q, i = pieces[n]
            return pltpu.make_async_copy(
                queries_ref.at[q, pl.ds(start + i * unit, unit)],
                held_ref.at[n % (ahead + 1)],
                sems.at[n % (ahead + 1)],
            )

        for n in range(ahead):
            copy(n).start()
        for n, (q, i) in enumerate(pieces):
            if n + ahead < len(pieces):
                copy(n + ahead).start()
            copy(n).wait()
            out_ref[q, :, pl.ds(i * unit, unit)] = lax.dot_general(
                acts_ref[...],
                held_ref[n % (ahead + 1)],
                (((1,), (1,)), ((), ())),
                preferred_element_type=F32,
            )

    return pl.pallas_call(
        kernel,
        in_specs=[VMEM, HBM],
        out_specs=VMEM,
        out_shape=jax.ShapeDtypeStruct((count, tokens, width), F32),
        scratch_shapes=[
            pltpu.VMEM((ahead + 1, unit, depth), BF16),
            pltpu.SemaphoreType.DMA((ahead + 1,)),
        ],
        compiler_params=limit(
            2 * depth * (tokens + (ahead + 1) * unit) + 4 * tokens * (count * width + unit)
        ),
        cost_estimate=pl.CostEstimate(
            flops=2 * count * tokens * depth * width,
            bytes_accessed=count * width * (2 * depth + 4 * tokens),
            transcendentals=0,
        ),
        name="project",
    )(rot_acts, *in_hbm([queries]))


def score(inner, own, inward, outward, projected):
    count, tokens, width = projected.shape
    unit = block_of(width, WIDE)

    def kernel(inner_ref, own_ref, *refs):
        outward_ref, projected_ref, out_ref = refs[-3:]

        @pl.when(pl.program_id(0) == 0)
        def _():
            out_ref[...] = jnp.zeros_like(out_ref)

        def add(total):
            for q in range(count):
                terms = projected_ref[q] * total
                part = terms[:, :LANES]
                for k in range(LANES, unit, LANES):
                    part = part + terms[:, k : k + LANES]
                out_ref[q] += part

        @pl.when(inner_ref[0] == 1)
        def _():
            total = own_ref[...]
            for r in refs[:-3]:
                total = total + r[...].astype(F32)
            add(total)

        @pl.when(inner_ref[0] == 0)
        def _():
            add(outward_ref[...].astype(F32))

    block = pl.BlockSpec((tokens, unit), lambda j: (0, j))
    return pl.pallas_call(
        kernel,
        grid=(width // unit,),
        in_specs=[pl.BlockSpec(memory_space=pltpu.SMEM)]
        + [block] * (len(inward) + 2)
        + [pl.BlockSpec((count, tokens, unit), lambda j: (0, 0, j))],
        out_specs=pl.BlockSpec((count, tokens, LANES), lambda j: (0, 0, 0)),
        out_shape=jax.ShapeDtypeStruct((count, tokens, LANES), F32),
        compiler_params=limit(2 * tokens * unit * (8 * count + 8 + 2 * len(inward))),
        cost_estimate=pl.CostEstimate(
            flops=2 * count * tokens * width,
            bytes_accessed=tokens * width * (4 * count + 6 + 2 * len(inward)),
            transcendentals=0,
        ),
        name="score",
    )(inner, own, *inward, outward, projected)


def line_steps(count):
    middle = count // 2
    inward = [[(s, s + 1), (count - 1 - s, count - 2 - s)] for s in range(middle - 1)]
    across = [(middle - 1, middle), (middle, middle - 1)]
    outward = [[(b, a) for a, b in pairs] for pairs in reversed(inward)]
    return inward + [across], outward


def chunks_of(size, count):
    unit = WIDE if size % WIDE == 0 else LANES
    units = size // unit
    most = -(-units // count)
    edges = [min(most * i, units) * unit for i in range(count + 1)]
    return [(a, b - a) for a, b in zip(edges, edges[1:]) if b > a]


def program(out_grads, acts, rot_out, rot_in, queries, token_sequence):
    tokens = token_sequence.shape[0]
    rows = lax.axis_size("row")
    col = Column("col")
    cols = col.count
    seqs, slots, features = out_grads.shape
    act_seqs = acts.shape[0]
    share = tokens // (rows * cols)

    held = [acts.reshape(act_seqs * slots, acts.shape[2])]
    for apart in range(1, rows):
        held.append(lax.ppermute(held[0], "row", [(i, i ^ apart) for i in range(rows)]))
    grads = col.gather(out_grads.reshape(seqs * slots, features))

    place = col.place(jnp.arange(cols, dtype=jnp.int32))
    order = place[:, None] == jnp.arange(cols, dtype=jnp.int32)[None, :]
    slot = token_slots(token_sequence, seqs * cols)
    grad_source = col.arrival(token_sequence // seqs) * seqs + token_sequence % seqs
    act_source = ((token_sequence // act_seqs) ^ lax.axis_index("row")) * act_seqs
    act_source = act_source + token_sequence % act_seqs

    def in_order(index):
        index = index.reshape(rows, cols, 1, share)
        index = jnp.where(order.reshape(1, cols, cols, 1), index, 0).sum(axis=1)
        return index.transpose(1, 0, 2).reshape(tokens)

    grad_pick = one_hot(in_order(grad_source * slots + slot), cols * seqs * slots)
    act_pick = one_hot(in_order(act_source * slots + slot), rows * act_seqs * slots)

    low, high = rotate_acts(act_pick, held, rot_in)
    packed = pack_rows(grad_pick, grads)

    inward, outward = line_steps(rows)
    chunks = []
    for start, width in chunks_of(rot_out.shape[1], CHUNKS):
        own, sent = rotate_grads(packed, rot_out, start, width)
        total, gots = own, []
        for pairs in inward:
            gots.append(lax.ppermute(sent, "row", pairs))
            total = total + gots[-1].astype(F32)
            sent = total.astype(BF16)
        chunks.append((start, width, own, gots, sent))

    rot_acts = col.spread(col.reduce(low, high).astype(BF16))

    z = lax.axis_index("row")
    inner = ((z == rows // 2 - 1) | (z == rows // 2)).astype(jnp.int32).reshape(1)
    scores = 0.0
    for start, width, own, gots, sent in chunks:
        projected = project(rot_acts, queries, start, width)
        back = sent
        for step, pairs in enumerate(outward):
            got = lax.ppermute(sent, "row", pairs)
            taken = (z == pairs[0][1]) | (z == pairs[1][1])
            back = got if step == 0 else jnp.where(taken, got, back)
            sent = back
        scores = scores + score(inner, own, gots, back, projected)

    count = scores.shape[0]
    scores = jnp.sum(scores, axis=2).reshape(count, 1, cols, rows, share)
    scores = jnp.sum(jnp.where(order.reshape(1, cols, cols, 1, 1), scores, 0.0), axis=2)
    spread = scores.transpose(2, 1, 0, 3).reshape(rows * cols, count * share)
    spread = lax.all_to_all(spread, ("row", "col"), 0, 0, tiled=True)
    return jnp.sum(spread, axis=0).reshape(count, share).T


def solution(mesh):
    placed = (
        P("col", None, "row"),
        P("row", None, "col"),
        P("row", "col"),
        P("col", "row"),
        P(None, "col", "row"),
        P(),
    )
    return jax.shard_map(
        program, mesh=mesh, in_specs=placed, out_specs=P(("row", "col"), None), check_vma=False
    )
```

time: 328 us -> 182 us (0.55)
  blocking collectives: 253 us -> 11.2 us
  waiting for transfers between devices: 0.73 us -> 68.6 us
  Pallas kernels: 0 us -> 49.8 us
  matrix products: 42.5 us -> 0 us
  starting transfers between devices: 0.01 us -> 40.6 us
  between operations: 13.5 us -> 0.55 us
  local copies, waits for them, and re-layouts: 13.1 us -> 4.85 us
    psum x2 -> x0, blocking collectives: 193 us -> none  [the longest x1 127 us: local(): lax.psum(jnp.dot(picked, rot_out, preferred_element_type=jnp.float32), 'r...]
    ppermute x0 -> x28, waiting for transfers between devices: none -> 68.6 us  [the longest x7 21.4 us: far(): lax.ppermute(value, self.axis, [(i, partner(i)) for i in range(self.count)])]
    pallas_call x0 -> x14, Pallas kernels: none -> 49.8 us  [the longest x4 22.6 us: rotate_grads(): pl.pallas_call(kernel, in_specs=[VMEM, HBM], out_specs=[VMEM, VMEM], out_...]
    dot_general x3 -> x0, matrix products: 42.5 us -> none  [the longest x1 24.3 us: local(): jnp.dot(picked, rot_out, preferred_element_type=jnp.float32)]
    ppermute x0 -> x28, starting transfers between devices: none -> 40.6 us  [the longest x8 15 us: program(): gots.append(lax.ppermute(sent, 'row', pairs))]
    unnamed x1 -> x0, blocking collectives: 39 us -> none
    all_gather x1 -> x0, blocking collectives: 21.5 us -> none  [local(): act_slots = lax.all_gather(acts, 'row', axis=0, tiled=True)]
    gather x2 -> x0, local copies, waits for them, and re-layouts: 12.5 us -> none  [the longest x1 11.3 us: local(): jnp.take(grad_slots.reshape(seq_count * slot_count, grad_slots.shape[2]),...]
  transfers between devices with their start and end apart: 1 -> 28, of which waited for: 0 -> 11; matrix products, arithmetic and copies ran while one was open for 2% -> 4% of each run, Pallas kernels for 0% -> 25%
where the time goes in v1:
time: 182 us; the launch traced here: 181 us
  waiting for transfers between devices  68.6 us (38%)
  Pallas kernels  49.8 us (27%)
  starting transfers between devices  40.6 us (22%)
  blocking collectives  11.2 us (6%)
  other arithmetic  5.79 us (3%)
  local copies, waits for them, and re-layouts  4.85 us (3%)
    pallas_call x4, Pallas kernels, rotate_grads(): pl.pallas_call(kernel, in_specs=[VMEM, HBM], out_specs=[VMEM, VMEM], out_...  22.6 us
    ppermute x7, waiting for transfers between devices, far(): lax.ppermute(value, self.axis, [(i, partner(i)) for i in range(self.count)])  21.4 us
    ppermute x4, waiting for transfers between devices, program(): got = lax.ppermute(sent, 'row', pairs)  17.7 us
    pallas_call x4, Pallas kernels, project(): pl.pallas_call(kernel, in_specs=[VMEM, HBM], out_specs=VMEM, out_shape=ja...  16.9 us
    ppermute x8, waiting for transfers between devices, program(): gots.append(lax.ppermute(sent, 'row', pairs))  16.6 us
    ppermute x8, starting transfers between devices, program(): gots.append(lax.ppermute(sent, 'row', pairs))  15 us
    ppermute x7, starting transfers between devices, far(): lax.ppermute(value, self.axis, [(i, partner(i)) for i in range(self.count)])  13.4 us
    ppermute x3, waiting for transfers between devices, program(): lax.ppermute(held[0], 'row', [(i, i ^ apart) for i in range(rows)])  11.9 us
  transfers between devices with their start and end apart: 28, of which 11 were waited for; matrix products, arithmetic and copies ran while one was open for 4% of the time, Pallas kernels for 25%

profile of v1, /device:TPU:0, one launch (start us, length us, event | category | flops | bytes accessed | tf_op | source)
XLA Modules:
  0.0 181.4 jit_solution(1959338174655376948)
XLA Ops:
  0.0 3.1 %collective-permute-start.10 = (bf16[96,1024]{1,0:T(8,128)(2,1)}, bf16[96,1024]{1,0:T(8,128)(2,1)S(1)}, u32[]{:S(2)}, u32[]{:S(2)}) collective-permute-start(bf16[96,1024]{1,0:T(8,128)(2,1)} %bitcast.7), channel_id=1, source_target_pairs={{0,8},{8,0},{16,24},{24,16},{1,9},{9,1},{17,25},{25,17},{2,10},{10... | collective-permute-start | bytes 589832 | tf_op jit(solution)/shard_map/ppermute | solution.py:393
  3.1 2.6 %collective-permute-start.11 = (bf16[96,1024]{1,0:T(8,128)(2,1)}, bf16[96,1024]{1,0:T(8,128)(2,1)S(1)}, u32[]{:S(2)}, u32[]{:S(2)}) collective-permute-start(bf16[96,1024]{1,0:T(8,128)(2,1)} %bitcast.8), channel_id=1, source_target_pairs={{0,16},{8,24},{16,0},{24,8},{1,17},{9,25},{17,1},{25,9},{2,18},{10... | collective-permute-start | bytes 589832 | tf_op jit(solution)/shard_map/ppermute | solution.py:393
  8.5 3.1 %collective-permute-done.10.refs_1_ = bf16[96,1024]{1,0:T(8,128)(2,1)S(1)} collective-permute-done((bf16[96,1024]{1,0:T(8,128)(2,1)}, bf16[96,1024]{1,0:T(8,128)(2,1)S(1)}, u32[]{:S(2)}, u32[]{:S(2)}) %collective-permute-start.10) | collective-permute-done | bytes 196640 | tf_op jit(solution)/shard_map/ppermute | solution.py:393
  11.6 8.7 %collective-permute-done.11.refs_2_ = bf16[96,1024]{1,0:T(8,128)(2,1)S(1)} collective-permute-done((bf16[96,1024]{1,0:T(8,128)(2,1)}, bf16[96,1024]{1,0:T(8,128)(2,1)S(1)}, u32[]{:S(2)}, u32[]{:S(2)}) %collective-permute-start.11) | collective-permute-done | bytes 196640 | tf_op jit(solution)/shard_map/ppermute | solution.py:393
  21.3 3.2 %rotate_acts.1 = (f32[128,2048]{1,0:T(8,128)S(1)}, f32[128,2048]{1,0:T(8,128)S(1)}) custom-call(bf16[256,384]{1,0:T(8,128)(2,1)S(1)} %fusion.4.onehot_ref, bf16[96,1024]{1,0:T(8,128)(2,1)S(1)} %bitcast.10, bf16[96,1024]{1,0:T(8,128)(2,1)S(1)} %collective-permute-done.10.refs_1_, bf16[96,1024]{1,0:T(8,128)(2,1)S(1)} %collective-permute-done.11.refs_2_, ...), custom_call_target="tpu_custom_call" | custom-call | flops 1275068416 | bytes 7077888 | tf_op jit(solution)/shard_map/rotate_acts/pallas_call | solution.py:246
  24.6 1.6 collective-permute-start
  27.4 1.6 collective-permute-start.14
  29.0 1.5 collective-permute-start.1
  30.5 9.3 %collective-permute-done.refs_1_ = bf16[48,7168]{1,0:T(8,128)(2,1)S(1)} collective-permute-done((bf16[48,7168]{1,0:T(8,128)(2,1)S(1)}, bf16[48,7168]{1,0:T(8,128)(2,1)S(1)}, u32[]{:S(2)}, u32[]{:S(2)}) %collective-permute-start) | collective-permute-done | bytes 688160 | tf_op jit(solution)/shard_map/ppermute | solution.py:41
  39.8 2.5 %collective-permute-start.2 = (bf16[48,7168]{1,0:T(8,128)(2,1)S(1)}, bf16[48,7168]{1,0:T(8,128)(2,1)S(1)}, u32[]{:S(2)}, u32[]{:S(2)}) collective-permute-start(bf16[48,7168]{1,0:T(8,128)(2,1)S(1)} %collective-permute-done.refs_1_), channel_id=1, source_target_pairs={{0,4},{1,3},{2,6},{3,1},{4,0},{5,7},{6,2},{7,5},{8,12},{9,11},{10,... | collective-permute-start | bytes 2064392 | tf_op jit(solution)/shard_map/ppermute | solution.py:41
  42.3 8.7 %collective-permute-done.14 = f32[64,2048]{1,0:T(8,128)S(1)} collective-permute-done((f32[64,2048]{1,0:T(8,128)S(1)}, f32[64,2048]{1,0:T(8,128)S(1)}, u32[]{:S(2)}, u32[]{:S(2)}) %collective-permute-start.14) | collective-permute-done | bytes 524320 | tf_op jit(solution)/shard_map/ppermute | solution.py:41
  51.9 2.5 %collective-permute-start.15 = (f32[32,2048]{1,0:T(8,128)}, f32[32,2048]{1,0:T(8,128)}, u32[]{:S(2)}, u32[]{:S(2)}) collective-permute-start(f32[32,2048]{1,0:T(8,128)} %slice.19), channel_id=1, source_target_pairs={{0,4},{1,3},{2,6},{3,1},{4,0},{5,7},{6,2},{7,5},{8,12},{9,11},{10,... | collective-permute-start | bytes 786440 | tf_op jit(solution)/shard_map/ppermute | solution.py:41
  55.9 3.1 %collective-permute-done.15 = f32[32,2048]{1,0:T(8,128)} collective-permute-done((f32[32,2048]{1,0:T(8,128)}, f32[32,2048]{1,0:T(8,128)}, u32[]{:S(2)}, u32[]{:S(2)}) %collective-permute-start.15) | collective-permute-done | bytes 262176 | tf_op jit(solution)/shard_map/ppermute | solution.py:41
  60.0 2.1 %collective-permute-start.16 = (bf16[32,2048]{1,0:T(8,128)(2,1)S(1)}, bf16[32,2048]{1,0:T(8,128)(2,1)S(1)}, u32[]{:S(2)}, u32[]{:S(2)}) collective-permute-start(bf16[32,2048]{1,0:T(8,128)(2,1)S(1)} %fusion.6), channel_id=1, source_target_pairs={{0,4},{1,3},{2,6},{3,1},{4,0},{5,7},{6,2},{7,5},{8,12},{9,11},{10,... | collective-permute-start | bytes 393224 | tf_op jit(solution)/shard_map/ppermute | solution.py:41
  64.1 5.0 %pack_grads.1.rows_ref = bf16[256,7168]{1,0:T(8,128)(2,1)S(1)} custom-call(bf16[256,384]{1,0:T(8,128)(2,1)S(1)} %fusion.3.onehot_ref, bf16[48,7168]{1,0:T(8,128)(2,1)} %bitcast.11, bf16[48,7168]{1,0:T(8,128)(2,1)} %copy-done.2, bf16[48,7168]{1,0:T(8,128)(2,1)} %copy-done.3, bf16[48,7168]{1,0:T(8,128)(2,1)} %copy-done.4, ...), custom_call_target="tpu_custom_call" | custom-call | flops 1409286144 | bytes 9175040 | tf_op jit(solution)/shard_map/pack_grads/pallas_call | solution.py:145
  69.1 6.2 %rotate_grads.5 = (f32[256,1024]{1,0:T(8,128)S(1)}, bf16[256,1024]{1,0:T(8,128)(2,1)S(1)}) custom-call(bf16[256,7168]{1,0:T(8,128)(2,1)S(1)} %pack_grads.1.rows_ref, bf16[7168,3584]{1,0:T(8,128)(2,1)} %basis_ref.7), custom_call_target="tpu_custom_call" | custom-call | flops 3758096384 | bytes 19922944 | tf_op jit(solution)/shard_map/rotate_grads/pallas_call | solution.py:198
  75.4 3.9 %rotate_grads.7 = (f32[256,512]{1,0:T(8,128)S(1)}, bf16[256,512]{1,0:T(8,128)(2,1)S(1)}) custom-call(bf16[256,7168]{1,0:T(8,128)(2,1)S(1)} %pack_grads.1.rows_ref, bf16[7168,3584]{1,0:T(8,128)(2,1)} %basis_ref.7), custom_call_target="tpu_custom_call" | custom-call | flops 1879048192 | bytes 11796480 | tf_op jit(solution)/shard_map/rotate_grads/pallas_call | solution.py:198
  79.2 5.3 %collective-permute-start.25 = (bf16[256,512]{1,0:T(8,128)(2,1)S(1)}, bf16[256,512]{1,0:T(8,128)(2,1)S(1)}, u32[]{:S(2)}, u32[]{:S(2)}) collective-permute-start(bf16[256,512]{1,0:T(8,128)(2,1)S(1)} %get-tuple-element.24), channel_id=1, source_target_pairs={{0,8},{24,16},{1,9},{25,17},{2,10},{26,18},{3,11},{27,19},{4,12},{... | collective-permute-start | bytes 786440 | tf_op jit(solution)/shard_map/ppermute | solution.py:420
  84.6 6.2 %rotate_grads.4 = (f32[256,1024]{1,0:T(8,128)S(1)}, bf16[256,1024]{1,0:T(8,128)(2,1)S(1)}) custom-call(bf16[256,7168]{1,0:T(8,128)(2,1)S(1)} %pack_grads.1.rows_ref, bf16[7168,3584]{1,0:T(8,128)(2,1)} %basis_ref.7), custom_call_target="tpu_custom_call" | custom-call | flops 3758096384 | bytes 19922944 | tf_op jit(solution)/shard_map/rotate_grads/pallas_call | solution.py:198
  92.4 1.6 collective-permute-start.17
  94.7 6.2 %rotate_grads.6 = (f32[256,1024]{1,0:T(8,128)S(1)}, bf16[256,1024]{1,0:T(8,128)(2,1)S(1)}) custom-call(bf16[256,7168]{1,0:T(8,128)(2,1)S(1)} %pack_grads.1.rows_ref, bf16[7168,3584]{1,0:T(8,128)(2,1)} %basis_ref.7), custom_call_target="tpu_custom_call" | custom-call | flops 3758096384 | bytes 19922944 | tf_op jit(solution)/shard_map/rotate_grads/pallas_call | solution.py:198
  100.9 4.1 %collective-permute-start.7 = (bf16[256,1024]{1,0:T(8,128)(2,1)S(1)}, bf16[256,1024]{1,0:T(8,128)(2,1)S(1)}, u32[]{:S(2)}, u32[]{:S(2)}) collective-permute-start(bf16[256,1024]{1,0:T(8,128)(2,1)S(1)} %get-tuple-element.16), channel_id=1, source_target_pairs={{0,8},{24,16},{1,9},{25,17},{2,10},{26,18},{3,11},{27,19},{4,12},{... | collective-permute-start | bytes 1572872 | tf_op jit(solution)/shard_map/ppermute | solution.py:420
  108.8 8.5 %collective-permute-done.7.refs_0_ = bf16[256,1024]{1,0:T(8,128)(2,1)S(1)} collective-permute-done((bf16[256,1024]{1,0:T(8,128)(2,1)S(1)}, bf16[256,1024]{1,0:T(8,128)(2,1)S(1)}, u32[]{:S(2)}, u32[]{:S(2)}) %collective-permute-start.7) | collective-permute-done | bytes 524320 | tf_op jit(solution)/shard_map/ppermute | solution.py:420
  118.1 8.0 %collective-permute-done.22.refs_0_ = bf16[256,1024]{1,0:T(8,128)(2,1)S(1)} collective-permute-done((bf16[256,1024]{1,0:T(8,128)(2,1)S(1)}, bf16[256,1024]{1,0:T(8,128)(2,1)S(1)}, u32[]{:S(2)}, u32[]{:S(2)}) %collective-permute-start.22) | collective-permute-done | bytes 524320 | tf_op jit(solution)/shard_map/ppermute | solution.py:420
  127.2 3.1 %project.7.refs_3_ = f32[2,256,512]{2,1,0:T(8,128)S(1)} custom-call(bf16[256,2048]{1,0:T(8,128)(2,1)S(1)} %pad_maximum_fusion.acts_ref, bf16[2,3584,2048]{2,1,0:T(8,128)(2,1)} %queries_ref.7), custom_call_target="tpu_custom_call" | custom-call | flops 1073741824 | bytes 5242880 | tf_op jit(solution)/shard_map/project/pallas_call | solution.py:296
  133.8 1.5 collective-permute-start.24
  135.4 4.6 %project.5.refs_3_ = f32[2,256,1024]{2,1,0:T(8,128)S(1)} custom-call(bf16[256,2048]{1,0:T(8,128)(2,1)S(1)} %pad_maximum_fusion.acts_ref, bf16[2,3584,2048]{2,1,0:T(8,128)(2,1)} %queries_ref.7), custom_call_target="tpu_custom_call" | custom-call | flops 2147483648 | bytes 10485760 | tf_op jit(solution)/shard_map/project/pallas_call | solution.py:296
  140.0 4.6 %project.4.refs_3_ = f32[2,256,1024]{2,1,0:T(8,128)S(1)} custom-call(bf16[256,2048]{1,0:T(8,128)(2,1)S(1)} %pad_maximum_fusion.acts_ref, bf16[2,3584,2048]{2,1,0:T(8,128)(2,1)} %queries_ref.7), custom_call_target="tpu_custom_call" | custom-call | flops 2147483648 | bytes 10485760 | tf_op jit(solution)/shard_map/project/pallas_call | solution.py:296
  144.6 4.6 %project.6.refs_3_ = f32[2,256,1024]{2,1,0:T(8,128)S(1)} custom-call(bf16[256,2048]{1,0:T(8,128)(2,1)S(1)} %pad_maximum_fusion.acts_ref, bf16[2,3584,2048]{2,1,0:T(8,128)(2,1)} %queries_ref.7), custom_call_target="tpu_custom_call" | custom-call | flops 2147483648 | bytes 10485760 | tf_op jit(solution)/shard_map/project/pallas_call | solution.py:296
  149.9 10.3 %collective-permute-done.9.refs_2_ = bf16[256,1024]{1,0:T(8,128)(2,1)S(1)} collective-permute-done((bf16[256,1024]{1,0:T(8,128)(2,1)S(1)}, bf16[256,1024]{1,0:T(8,128)(2,1)S(1)}, u32[]{:S(2)}, u32[]{:S(2)}) %collective-permute-start.9) | collective-permute-done | bytes 524320 | tf_op jit(solution)/shard_map/ppermute | solution.py:434
  160.9 7.4 %collective-permute-done.24.refs_2_ = bf16[256,1024]{1,0:T(8,128)(2,1)S(1)} collective-permute-done((bf16[256,1024]{1,0:T(8,128)(2,1)S(1)}, bf16[256,1024]{1,0:T(8,128)(2,1)S(1)}, u32[]{:S(2)}, u32[]{:S(2)}) %collective-permute-start.24) | collective-permute-done | bytes 524320 | tf_op jit(solution)/shard_map/ppermute | solution.py:434
  169.5 11.2 %all_to_all.9 = f32[32,1,16]{2,1,0:T(1,128)S(1)} all-to-all(f32[32,1,16]{2,1,0:T(1,128)S(1)} %reshape.101), channel_id=1, replica_groups=mesh['row'=4,'col'=8] {'row','col'}, dimensions={0} | all-to-all | bytes 4096 | tf_op jit(solution)/shard_map/all_to_all | solution.py:444
  (93 shorter events, 24.8 us)
Async XLA Ops:
  0.0 11.6 %collective-permute-start.10 = (bf16[96,1024]{1,0:T(8,128)(2,1)}, bf16[96,1024]{1,0:T(8,128)(2,1)S(1)}, u32[]{:S(2)}, u32[]{:S(2)}) collective-permute-start(bf16[96,1024]{1,0:T(8,128)(2,1)} %bitcast.7), channel_id=1, source_target_pairs={{0,8},{8,0},{16,24},{24,16},{1,9},{9,1},{17,25},{25,17},{2,10},{10... | collective-permute-start | bytes 589832 | tf_op jit(solution)/shard_map/ppermute | solution.py:393
  3.1 17.3 %collective-permute-start.11 = (bf16[96,1024]{1,0:T(8,128)(2,1)}, bf16[96,1024]{1,0:T(8,128)(2,1)S(1)}, u32[]{:S(2)}, u32[]{:S(2)}) collective-permute-start(bf16[96,1024]{1,0:T(8,128)(2,1)} %bitcast.8), channel_id=1, source_target_pairs={{0,16},{8,24},{16,0},{24,8},{1,17},{9,25},{17,1},{25,9},{2,18},{10... | collective-permute-start | bytes 589832 | tf_op jit(solution)/shard_map/ppermute | solution.py:393
  5.6 14.7 %collective-permute-start.12 = (bf16[96,1024]{1,0:T(8,128)(2,1)}, bf16[96,1024]{1,0:T(8,128)(2,1)S(1)}, u32[]{:S(2)}, u32[]{:S(2)}) collective-permute-start(bf16[96,1024]{1,0:T(8,128)(2,1)} %bitcast.9), channel_id=1, source_target_pairs={{0,24},{8,16},{16,8},{24,0},{1,25},{9,17},{17,9},{25,1},{2,26},{10... | collective-permute-start | bytes 589832 | tf_op jit(solution)/shard_map/ppermute | solution.py:393
  21.3 3.3 %copy-start.1 = (bf16[1,48,7168]{2,1,0:T(8,128)(2,1)S(1)}, bf16[1,48,7168]{2,1,0:T(8,128)(2,1)}, u32[]{:S(2)}) copy-start(bf16[1,48,7168]{2,1,0:T(8,128)(2,1)} %param.6) | copy-start | bytes 2064388
  24.5 2.7 %collective-permute-start.13 = (f32[128,2048]{1,0:T(8,128)S(1)}, f32[128,2048]{1,0:T(8,128)S(1)}, u32[]{:S(2)}, u32[]{:S(2)}) collective-permute-start(f32[128,2048]{1,0:T(8,128)S(1)} %get-tuple-element.18), channel_id=1, source_target_pairs={{0,1},{1,0},{2,3},{3,2},{4,5},{5,4},{6,7},{7,6},{8,9},{9,8},{10,11... | collective-permute-start | bytes 3145736 | tf_op jit(solution)/shard_map/ppermute | solution.py:35
  24.6 15.2 %collective-permute-start = (bf16[48,7168]{1,0:T(8,128)(2,1)S(1)}, bf16[48,7168]{1,0:T(8,128)(2,1)S(1)}, u32[]{:S(2)}, u32[]{:S(2)}) collective-permute-start(bf16[48,7168]{1,0:T(8,128)(2,1)S(1)} %bitcast.12), channel_id=1, source_target_pairs={{0,2},{1,5},{2,0},{3,7},{4,6},{5,1},{6,4},{7,3},{8,10},{9,13},{10,... | collective-permute-start | bytes 2064392 | tf_op jit(solution)/shard_map/ppermute | solution.py:41
  27.4 23.6 %collective-permute-start.14 = (f32[64,2048]{1,0:T(8,128)S(1)}, f32[64,2048]{1,0:T(8,128)S(1)}, u32[]{:S(2)}, u32[]{:S(2)}) collective-permute-start(f32[64,2048]{1,0:T(8,128)S(1)} %slice.17), channel_id=1, source_target_pairs={{0,2},{1,5},{2,0},{3,7},{4,6},{5,1},{6,4},{7,3},{8,10},{9,13},{10,... | collective-permute-start | bytes 1572872 | tf_op jit(solution)/shard_map/ppermute | solution.py:41
  29.0 26.1 %collective-permute-start.1 = (bf16[48,7168]{1,0:T(8,128)(2,1)S(1)}, bf16[48,7168]{1,0:T(8,128)(2,1)S(1)}, u32[]{:S(2)}, u32[]{:S(2)}) collective-permute-start(bf16[48,7168]{1,0:T(8,128)(2,1)S(1)} %bitcast.13), channel_id=1, source_target_pairs={{0,4},{1,3},{2,6},{3,1},{4,0},{5,7},{6,2},{7,5},{8,12},{9,11},{10,... | collective-permute-start | bytes 2064392 | tf_op jit(solution)/shard_map/ppermute | solution.py:41
  39.8 22.4 %copy-start.2 = (bf16[48,7168]{1,0:T(8,128)(2,1)}, bf16[48,7168]{1,0:T(8,128)(2,1)S(1)}, u32[]{:S(2)}) copy-start(bf16[48,7168]{1,0:T(8,128)(2,1)S(1)} %collective-permute-done.refs_1_) | copy-start | bytes 2064388
  39.8 15.7 %collective-permute-start.2 = (bf16[48,7168]{1,0:T(8,128)(2,1)S(1)}, bf16[48,7168]{1,0:T(8,128)(2,1)S(1)}, u32[]{:S(2)}, u32[]{:S(2)}) collective-permute-start(bf16[48,7168]{1,0:T(8,128)(2,1)S(1)} %collective-permute-done.refs_1_), channel_id=1, source_target_pairs={{0,4},{1,3},{2,6},{3,1},{4,0},{5,7},{6,2},{7,5},{8,12},{9,11},{10,... | collective-permute-start | bytes 2064392 | tf_op jit(solution)/shard_map/ppermute | solution.py:41
  51.9 7.2 %collective-permute-start.15 = (f32[32,2048]{1,0:T(8,128)}, f32[32,2048]{1,0:T(8,128)}, u32[]{:S(2)}, u32[]{:S(2)}) collective-permute-start(f32[32,2048]{1,0:T(8,128)} %slice.19), channel_id=1, source_target_pairs={{0,4},{1,3},{2,6},{3,1},{4,0},{5,7},{6,2},{7,5},{8,12},{9,11},{10,... | collective-permute-start | bytes 786440 | tf_op jit(solution)/shard_map/ppermute | solution.py:41
  54.4 7.7 %collective-permute-start.3 = (bf16[48,7168]{1,0:T(8,128)(2,1)S(1)}, bf16[48,7168]{1,0:T(8,128)(2,1)}, u32[]{:S(2)}, u32[]{:S(2)}) collective-permute-start(bf16[48,7168]{1,0:T(8,128)(2,1)S(1)} %bitcast.14), channel_id=1, source_target_pairs={{0,1},{1,0},{2,3},{3,2},{4,5},{5,4},{6,7},{7,6},{8,9},{9,8},{10,11... | collective-permute-start | bytes 2064392 | tf_op jit(solution)/shard_map/ppermute | solution.py:35
  54.5 7.6 %collective-permute-start.4 = (bf16[48,7168]{1,0:T(8,128)(2,1)S(1)}, bf16[48,7168]{1,0:T(8,128)(2,1)S(1)}, u32[]{:S(2)}, u32[]{:S(2)}) collective-permute-start(bf16[48,7168]{1,0:T(8,128)(2,1)S(1)} %collective-permute-done.refs_1_), channel_id=1, source_target_pairs={{0,1},{1,0},{2,3},{3,2},{4,5},{5,4},{6,7},{7,6},{8,9},{9,8},{10,11... | collective-permute-start | bytes 2064392 | tf_op jit(solution)/shard_map/ppermute | solution.py:35
  55.1 7.1 %copy-start.3 = (bf16[48,7168]{1,0:T(8,128)(2,1)}, bf16[48,7168]{1,0:T(8,128)(2,1)S(1)}, u32[]{:S(2)}) copy-start(bf16[48,7168]{1,0:T(8,128)(2,1)S(1)} %collective-permute-done.1.refs_2_) | copy-start | bytes 2064388
  55.1 7.1 %collective-permute-start.5 = (bf16[48,7168]{1,0:T(8,128)(2,1)S(1)}, bf16[48,7168]{1,0:T(8,128)(2,1)S(1)}, u32[]{:S(2)}, u32[]{:S(2)}) collective-permute-start(bf16[48,7168]{1,0:T(8,128)(2,1)S(1)} %collective-permute-done.1.refs_2_), channel_id=1, source_target_pairs={{0,1},{1,0},{2,3},{3,2},{4,5},{5,4},{6,7},{7,6},{8,9},{9,8},{10,11... | collective-permute-start | bytes 2064392 | tf_op jit(solution)/shard_map/ppermute | solution.py:35
  55.5 6.7 %copy-start.4 = (bf16[48,7168]{1,0:T(8,128)(2,1)}, bf16[48,7168]{1,0:T(8,128)(2,1)S(1)}, u32[]{:S(2)}) copy-start(bf16[48,7168]{1,0:T(8,128)(2,1)S(1)} %collective-permute-done.2.refs_3_) | copy-start | bytes 2064388
  55.5 6.7 %collective-permute-start.6 = (bf16[48,7168]{1,0:T(8,128)(2,1)S(1)}, bf16[48,7168]{1,0:T(8,128)(2,1)S(1)}, u32[]{:S(2)}, u32[]{:S(2)}) collective-permute-start(bf16[48,7168]{1,0:T(8,128)(2,1)S(1)} %collective-permute-done.2.refs_3_), channel_id=1, source_target_pairs={{0,1},{1,0},{2,3},{3,2},{4,5},{5,4},{6,7},{7,6},{8,9},{9,8},{10,11... | collective-permute-start | bytes 2064392 | tf_op jit(solution)/shard_map/ppermute | solution.py:35
  60.0 32.3 %collective-permute-start.16 = (bf16[32,2048]{1,0:T(8,128)(2,1)S(1)}, bf16[32,2048]{1,0:T(8,128)(2,1)S(1)}, u32[]{:S(2)}, u32[]{:S(2)}) collective-permute-start(bf16[32,2048]{1,0:T(8,128)(2,1)S(1)} %fusion.6), channel_id=1, source_target_pairs={{0,4},{1,3},{2,6},{3,1},{4,0},{5,7},{6,2},{7,5},{8,12},{9,11},{10,... | collective-permute-start | bytes 393224 | tf_op jit(solution)/shard_map/ppermute | solution.py:41
  79.2 14.7 %collective-permute-start.25 = (bf16[256,512]{1,0:T(8,128)(2,1)S(1)}, bf16[256,512]{1,0:T(8,128)(2,1)S(1)}, u32[]{:S(2)}, u32[]{:S(2)}) collective-permute-start(bf16[256,512]{1,0:T(8,128)(2,1)S(1)} %get-tuple-element.24), channel_id=1, source_target_pairs={{0,8},{24,16},{1,9},{25,17},{2,10},{26,18},{3,11},{27,19},{4,12},{... | collective-permute-start | bytes 786440 | tf_op jit(solution)/shard_map/ppermute | solution.py:420
  90.8 17.1 %collective-permute-start.19 = (bf16[256,1024]{1,0:T(8,128)(2,1)S(1)}, bf16[256,1024]{1,0:T(8,128)(2,1)S(1)}, u32[]{:S(2)}, u32[]{:S(2)}) collective-permute-start(bf16[256,1024]{1,0:T(8,128)(2,1)S(1)} %get-tuple-element.20), channel_id=1, source_target_pairs={{0,8},{24,16},{1,9},{25,17},{2,10},{26,18},{3,11},{27,19},{4,12},{... | collective-permute-start | bytes 1572872 | tf_op jit(solution)/shard_map/ppermute | solution.py:420
  92.4 14.0 %collective-permute-start.17 = (bf16[64,2048]{1,0:T(8,128)(2,1)S(1)}, bf16[64,2048]{1,0:T(8,128)(2,1)S(1)}, u32[]{:S(2)}, u32[]{:S(2)}) collective-permute-start(bf16[64,2048]{1,0:T(8,128)(2,1)S(1)} %pad_maximum_fusion.2), channel_id=1, source_target_pairs={{0,2},{1,5},{2,0},{3,7},{4,6},{5,1},{6,4},{7,3},{8,10},{9,13},{10,... | collective-permute-start | bytes 786440 | tf_op jit(solution)/shard_map/ppermute | solution.py:41
  94.0 12.5 %collective-permute-start.26 = (bf16[256,512]{1,0:T(8,128)(2,1)S(1)}, bf16[256,512]{1,0:T(8,128)(2,1)S(1)}, u32[]{:S(2)}, u32[]{:S(2)}) collective-permute-start(bf16[256,512]{1,0:T(8,128)(2,1)S(1)} %fusion.5), channel_id=1, source_target_pairs={{8,16},{16,8},{9,17},{17,9},{10,18},{18,10},{11,19},{19,11},{12,20... | collective-permute-start | bytes 786440 | tf_op jit(solution)/shard_map/ppermute | solution.py:420
  100.9 16.3 %collective-permute-start.7 = (bf16[256,1024]{1,0:T(8,128)(2,1)S(1)}, bf16[256,1024]{1,0:T(8,128)(2,1)S(1)}, u32[]{:S(2)}, u32[]{:S(2)}) collective-permute-start(bf16[256,1024]{1,0:T(8,128)(2,1)S(1)} %get-tuple-element.16), channel_id=1, source_target_pairs={{0,8},{24,16},{1,9},{25,17},{2,10},{26,18},{3,11},{27,19},{4,12},{... | collective-permute-start | bytes 1572872 | tf_op jit(solution)/shard_map/ppermute | solution.py:420
  105.0 21.2 %collective-permute-start.22 = (bf16[256,1024]{1,0:T(8,128)(2,1)S(1)}, bf16[256,1024]{1,0:T(8,128)(2,1)S(1)}, u32[]{:S(2)}, u32[]{:S(2)}) collective-permute-start(bf16[256,1024]{1,0:T(8,128)(2,1)S(1)} %get-tuple-element.22), channel_id=1, source_target_pairs={{0,8},{24,16},{1,9},{25,17},{2,10},{26,18},{3,11},{27,19},{4,12},{... | collective-permute-start | bytes 1572872 | tf_op jit(solution)/shard_map/ppermute | solution.py:420
  106.4 20.6 %collective-permute-start.18 = (bf16[128,2048]{1,0:T(8,128)(2,1)S(1)}, bf16[128,2048]{1,0:T(8,128)(2,1)S(1)}, u32[]{:S(2)}, u32[]{:S(2)}) collective-permute-start(bf16[128,2048]{1,0:T(8,128)(2,1)S(1)} %pad_maximum_fusion.1), channel_id=1, source_target_pairs={{0,1},{1,0},{2,3},{3,2},{4,5},{5,4},{6,7},{7,6},{8,9},{9,8},{10,11... | collective-permute-start | bytes 1572872 | tf_op jit(solution)/shard_map/ppermute | solution.py:35
  106.6 23.7 %collective-permute-start.27 = (bf16[256,512]{1,0:T(8,128)(2,1)S(1)}, bf16[256,512]{1,0:T(8,128)(2,1)S(1)}, u32[]{:S(2)}, u32[]{:S(2)}) collective-permute-start(bf16[256,512]{1,0:T(8,128)(2,1)S(1)} %add_convert_fusion.3), channel_id=1, source_target_pairs={{8,0},{16,24},{9,1},{17,25},{10,2},{18,26},{11,3},{19,27},{12,4},{... | collective-permute-start | bytes 786440 | tf_op jit(solution)/shard_map/ppermute | solution.py:434
  108.1 22.4 %collective-permute-start.20 = (bf16[256,1024]{1,0:T(8,128)(2,1)S(1)}, bf16[256,1024]{1,0:T(8,128)(2,1)S(1)}, u32[]{:S(2)}, u32[]{:S(2)}) collective-permute-start(bf16[256,1024]{1,0:T(8,128)(2,1)S(1)} %fusion.1), channel_id=1, source_target_pairs={{8,16},{16,8},{9,17},{17,9},{10,18},{18,10},{11,19},{19,11},{12,20... | collective-permute-start | bytes 1572872 | tf_op jit(solution)/shard_map/ppermute | solution.py:420
  117.4 14.6 %collective-permute-start.8 = (bf16[256,1024]{1,0:T(8,128)(2,1)S(1)}, bf16[256,1024]{1,0:T(8,128)(2,1)S(1)}, u32[]{:S(2)}, u32[]{:S(2)}) collective-permute-start(bf16[256,1024]{1,0:T(8,128)(2,1)S(1)} %fusion), channel_id=1, source_target_pairs={{8,16},{16,8},{9,17},{17,9},{10,18},{18,10},{11,19},{19,11},{12,20... | collective-permute-start | bytes 1572872 | tf_op jit(solution)/shard_map/ppermute | solution.py:420
  126.3 7.2 %collective-permute-start.23 = (bf16[256,1024]{1,0:T(8,128)(2,1)S(1)}, bf16[256,1024]{1,0:T(8,128)(2,1)S(1)}, u32[]{:S(2)}, u32[]{:S(2)}) collective-permute-start(bf16[256,1024]{1,0:T(8,128)(2,1)S(1)} %fusion.2), channel_id=1, source_target_pairs={{8,16},{16,8},{9,17},{17,9},{10,18},{18,10},{11,19},{19,11},{12,20... | collective-permute-start | bytes 1572872 | tf_op jit(solution)/shard_map/ppermute | solution.py:420
  130.7 18.5 %collective-permute-start.21 = (bf16[256,1024]{1,0:T(8,128)(2,1)S(1)}, bf16[256,1024]{1,0:T(8,128)(2,1)S(1)}, u32[]{:S(2)}, u32[]{:S(2)}) collective-permute-start(bf16[256,1024]{1,0:T(8,128)(2,1)S(1)} %add_convert_fusion.1), channel_id=1, source_target_pairs={{8,0},{16,24},{9,1},{17,25},{10,2},{18,26},{11,3},{19,27},{12,4},{... | collective-permute-start | bytes 1572872 | tf_op jit(solution)/shard_map/ppermute | solution.py:434
  132.3 27.9 %collective-permute-start.9 = (bf16[256,1024]{1,0:T(8,128)(2,1)S(1)}, bf16[256,1024]{1,0:T(8,128)(2,1)S(1)}, u32[]{:S(2)}, u32[]{:S(2)}) collective-permute-start(bf16[256,1024]{1,0:T(8,128)(2,1)S(1)} %add_convert_fusion.2), channel_id=1, source_target_pairs={{8,0},{16,24},{9,1},{17,25},{10,2},{18,26},{11,3},{19,27},{12,4},{... | collective-permute-start | bytes 1572872 | tf_op jit(solution)/shard_map/ppermute | solution.py:434
  133.8 34.4 %collective-permute-start.24 = (bf16[256,1024]{1,0:T(8,128)(2,1)S(1)}, bf16[256,1024]{1,0:T(8,128)(2,1)S(1)}, u32[]{:S(2)}, u32[]{:S(2)}) collective-permute-start(bf16[256,1024]{1,0:T(8,128)(2,1)S(1)} %add_convert_fusion), channel_id=1, source_target_pairs={{8,0},{16,24},{9,1},{17,25},{10,2},{18,26},{11,3},{19,27},{12,4},{... | collective-permute-start | bytes 1572872 | tf_op jit(solution)/shard_map/ppermute | solution.py:434
  (4 other events, 3.7 us)

commit v2 on v1

--- a/solution.py
+++ b/solution.py
@@ -9,7 +9,7 @@
 BF16 = jnp.bfloat16
 LANES = 128
 WIDE = 512
-CHUNKS = 4
+PARTS = (2, 2, 2, 1)
 
 
 def block_of(size, limit):
@@ -314,53 +314,39 @@
     )(rot_acts, *in_hbm([queries]))
 
 
-def score(inner, own, inward, outward, projected):
+def score(inner, kept, outward, projected):
     count, tokens, width = projected.shape
     unit = block_of(width, WIDE)
 
-    def kernel(inner_ref, own_ref, *refs):
-        outward_ref, projected_ref, out_ref = refs[-3:]
-
-        @pl.when(pl.program_id(0) == 0)
-        def _():
-            out_ref[...] = jnp.zeros_like(out_ref)
-
-        def add(total):
+    def kernel(inner_ref, kept_ref, outward_ref, projected_ref, out_ref):
+        def add(total_ref):
+            parts = [None] * count
+            for at in range(0, width, unit):
+                total = total_ref[:, pl.ds(at, unit)].astype(F32)
+                for q in range(count):
+                    terms = projected_ref[q, :, pl.ds(at, unit)] * total
+                    for k in range(0, unit, LANES):
+                        term = terms[:, k : k + LANES]
+                        parts[q] = term if parts[q] is None else parts[q] + term
             for q in range(count):
-                terms = projected_ref[q] * total
-                part = terms[:, :LANES]
-                for k in range(LANES, unit, LANES):
-                    part = part + terms[:, k : k + LANES]
-                out_ref[q] += part
-
-        @pl.when(inner_ref[0] == 1)
-        def _():
-            total = own_ref[...]
-            for r in refs[:-3]:
-                total = total + r[...].astype(F32)
-            add(total)
-
-        @pl.when(inner_ref[0] == 0)
-        def _():
-            add(outward_ref[...].astype(F32))
-
-    block = pl.BlockSpec((tokens, unit), lambda j: (0, j))
+                out_ref[q] = parts[q]
+
+        pl.when(inner_ref[0] == 1)(lambda: add(kept_ref))
+        pl.when(inner_ref[0] == 0)(lambda: add(outward_ref))
+
     return pl.pallas_call(
         kernel,
-        grid=(width // unit,),
-        in_specs=[pl.BlockSpec(memory_space=pltpu.SMEM)]
-        + [block] * (len(inward) + 2)
-        + [pl.BlockSpec((count, tokens, unit), lambda j: (0, 0, j))],
-        out_specs=pl.BlockSpec((count, tokens, LANES), lambda j: (0, 0, 0)),
+        in_specs=[pl.BlockSpec(memory_space=pltpu.SMEM)] + [VMEM] * 3,
+        out_specs=VMEM,
         out_shape=jax.ShapeDtypeStruct((count, tokens, LANES), F32),
-        compiler_params=limit(2 * tokens * unit * (8 * count + 8 + 2 * len(inward))),
+        compiler_params=limit(tokens * (width * (4 * count + 4) + 8 * count * LANES + 8 * unit)),
         cost_estimate=pl.CostEstimate(
             flops=2 * count * tokens * width,
-            bytes_accessed=tokens * width * (4 * count + 6 + 2 * len(inward)),
+            bytes_accessed=tokens * width * (4 * count + 4),
             transcendentals=0,
         ),
         name="score",
-    )(inner, own, *inward, outward, projected)
+    )(inner, kept, outward, projected)
 
 
 def line_steps(count):
@@ -371,12 +357,11 @@
     return inward + [across], outward
 
 
-def chunks_of(size, count):
+def chunks_of(size):
     unit = WIDE if size % WIDE == 0 else LANES
     units = size // unit
-    most = -(-units // count)
-    edges = [min(most * i, units) * unit for i in range(count + 1)]
-    return [(a, b - a) for a, b in zip(edges, edges[1:]) if b > a]
+    edges = [sum(PARTS[:k]) * units // sum(PARTS) * unit for k in range(len(PARTS) + 1)]
+    return [(a, b - a) for a, b in zip(edges, edges[1:])]
 
 
 def program(out_grads, acts, rot_out, rot_in, queries, token_sequence):
@@ -413,29 +398,28 @@
 
     inward, outward = line_steps(rows)
     chunks = []
-    for start, width in chunks_of(rot_out.shape[1], CHUNKS):
+    for start, width in chunks_of(rot_out.shape[1]):
         own, sent = rotate_grads(packed, rot_out, start, width)
-        total, gots = own, []
+        total = own
         for pairs in inward:
-            gots.append(lax.ppermute(sent, "row", pairs))
-            total = total + gots[-1].astype(F32)
+            total = total + lax.ppermute(sent, "row", pairs).astype(F32)
             sent = total.astype(BF16)
-        chunks.append((start, width, own, gots, sent))
+        chunks.append((start, width, sent))
 
     rot_acts = col.spread(col.reduce(low, high).astype(BF16))
 
     z = lax.axis_index("row")
     inner = ((z == rows // 2 - 1) | (z == rows // 2)).astype(jnp.int32).reshape(1)
     scores = 0.0
-    for start, width, own, gots, sent in chunks:
+    for start, width, sent in chunks:
         projected = project(rot_acts, queries, start, width)
-        back = sent
+        kept = back = sent
         for step, pairs in enumerate(outward):
             got = lax.ppermute(sent, "row", pairs)
             taken = (z == pairs[0][1]) | (z == pairs[1][1])
             back = got if step == 0 else jnp.where(taken, got, back)
             sent = back
-        scores = scores + score(inner, own, gots, back, projected)
+        scores = scores + score(inner, kept, back, projected)
 
     count = scores.shape[0]
     scores = jnp.sum(scores, axis=2).reshape(count, 1, cols, rows, share)

time: 182 us -> 181 us (level)
  no operation moved by 1% of the time
where the time goes in v2:
time: 181 us
  waiting for transfers between devices  69.4 us (38%)
  Pallas kernels  48.5 us (27%)
  starting transfers between devices  40.6 us (22%)
  blocking collectives  11.2 us (6%)
  other arithmetic  5.78 us (3%)
  local copies, waits for them, and re-layouts  4.85 us (3%)
    pallas_call x4, Pallas kernels, rotate_grads(): pl.pallas_call(kernel, in_specs=[VMEM, HBM], out_specs=[VMEM, VMEM], out_...  22.6 us
    ppermute x7, waiting for transfers between devices, far(): lax.ppermute(value, self.axis, [(i, partner(i)) for i in range(self.count)])  21.4 us
    ppermute x4, waiting for transfers between devices, program(): got = lax.ppermute(sent, 'row', pairs)  18.5 us
    pallas_call x4, Pallas kernels, project(): pl.pallas_call(kernel, in_specs=[VMEM, HBM], out_specs=VMEM, out_shape=ja...  16.9 us
    ppermute x8, waiting for transfers between devices, program(): total = total + lax.ppermute(sent, 'row', pairs).astype(F32)  16.5 us
    ppermute x8, starting transfers between devices, program(): total = total + lax.ppermute(sent, 'row', pairs).astype(F32)  15 us
    ppermute x7, starting transfers between devices, far(): lax.ppermute(value, self.axis, [(i, partner(i)) for i in range(self.count)])  13.4 us
    ppermute x3, waiting for transfers between devices, program(): lax.ppermute(held[0], 'row', [(i, i ^ apart) for i in range(rows)])  11.9 us
  transfers between devices with their start and end apart: 28, of which 11 were waited for; matrix products, arithmetic and copies ran while one was open for 4% of the time, Pallas kernels for 25%

profile of v2, /device:TPU:0, one launch (start us, length us, event | category | flops | bytes accessed | tf_op | source)
XLA Modules:
  0.0 180.8 jit_solution(7476003821188328315)
XLA Ops:
  0.0 3.1 %collective-permute-start.10 = (bf16[96,1024]{1,0:T(8,128)(2,1)}, bf16[96,1024]{1,0:T(8,128)(2,1)S(1)}, u32[]{:S(2)}, u32[]{:S(2)}) collective-permute-start(bf16[96,1024]{1,0:T(8,128)(2,1)} %bitcast.7), channel_id=1, source_target_pairs={{0,8},{8,0},{16,24},{24,16},{1,9},{9,1},{17,25},{25,17},{2,10},{10... | collective-permute-start | bytes 589832 | tf_op jit(solution)/shard_map/ppermute | solution.py:378
  3.1 2.6 %collective-permute-start.11 = (bf16[96,1024]{1,0:T(8,128)(2,1)}, bf16[96,1024]{1,0:T(8,128)(2,1)S(1)}, u32[]{:S(2)}, u32[]{:S(2)}) collective-permute-start(bf16[96,1024]{1,0:T(8,128)(2,1)} %bitcast.8), channel_id=1, source_target_pairs={{0,16},{8,24},{16,0},{24,8},{1,17},{9,25},{17,1},{25,9},{2,18},{10... | collective-permute-start | bytes 589832 | tf_op jit(solution)/shard_map/ppermute | solution.py:378
  8.5 3.1 %collective-permute-done.10.refs_1_ = bf16[96,1024]{1,0:T(8,128)(2,1)S(1)} collective-permute-done((bf16[96,1024]{1,0:T(8,128)(2,1)}, bf16[96,1024]{1,0:T(8,128)(2,1)S(1)}, u32[]{:S(2)}, u32[]{:S(2)}) %collective-permute-start.10) | collective-permute-done | bytes 196640 | tf_op jit(solution)/shard_map/ppermute | solution.py:378
  11.6 8.7 %collective-permute-done.11.refs_2_ = bf16[96,1024]{1,0:T(8,128)(2,1)S(1)} collective-permute-done((bf16[96,1024]{1,0:T(8,128)(2,1)}, bf16[96,1024]{1,0:T(8,128)(2,1)S(1)}, u32[]{:S(2)}, u32[]{:S(2)}) %collective-permute-start.11) | collective-permute-done | bytes 196640 | tf_op jit(solution)/shard_map/ppermute | solution.py:378
  21.3 3.2 %rotate_acts.1 = (f32[128,2048]{1,0:T(8,128)S(1)}, f32[128,2048]{1,0:T(8,128)S(1)}) custom-call(bf16[256,384]{1,0:T(8,128)(2,1)S(1)} %fusion.4.onehot_ref, bf16[96,1024]{1,0:T(8,128)(2,1)S(1)} %bitcast.10, bf16[96,1024]{1,0:T(8,128)(2,1)S(1)} %collective-permute-done.10.refs_1_, bf16[96,1024]{1,0:T(8,128)(2,1)S(1)} %collective-permute-done.11.refs_2_, ...), custom_call_target="tpu_custom_call" | custom-call | flops 1275068416 | bytes 7077888 | tf_op jit(solution)/shard_map/rotate_acts/pallas_call | solution.py:246
  24.6 1.6 collective-permute-start
  27.4 1.6 collective-permute-start.14
  29.0 1.5 collective-permute-start.1
  30.5 9.3 %collective-permute-done.refs_1_ = bf16[48,7168]{1,0:T(8,128)(2,1)S(1)} collective-permute-done((bf16[48,7168]{1,0:T(8,128)(2,1)S(1)}, bf16[48,7168]{1,0:T(8,128)(2,1)S(1)}, u32[]{:S(2)}, u32[]{:S(2)}) %collective-permute-start) | collective-permute-done | bytes 688160 | tf_op jit(solution)/shard_map/ppermute | solution.py:41
  39.8 2.5 %collective-permute-start.2 = (bf16[48,7168]{1,0:T(8,128)(2,1)S(1)}, bf16[48,7168]{1,0:T(8,128)(2,1)S(1)}, u32[]{:S(2)}, u32[]{:S(2)}) collective-permute-start(bf16[48,7168]{1,0:T(8,128)(2,1)S(1)} %collective-permute-done.refs_1_), channel_id=1, source_target_pairs={{0,4},{1,3},{2,6},{3,1},{4,0},{5,7},{6,2},{7,5},{8,12},{9,11},{10,... | collective-permute-start | bytes 2064392 | tf_op jit(solution)/shard_map/ppermute | solution.py:41
  42.3 8.7 %collective-permute-done.14 = f32[64,2048]{1,0:T(8,128)S(1)} collective-permute-done((f32[64,2048]{1,0:T(8,128)S(1)}, f32[64,2048]{1,0:T(8,128)S(1)}, u32[]{:S(2)}, u32[]{:S(2)}) %collective-permute-start.14) | collective-permute-done | bytes 524320 | tf_op jit(solution)/shard_map/ppermute | solution.py:41
  51.9 2.5 %collective-permute-start.15 = (f32[32,2048]{1,0:T(8,128)}, f32[32,2048]{1,0:T(8,128)}, u32[]{:S(2)}, u32[]{:S(2)}) collective-permute-start(f32[32,2048]{1,0:T(8,128)} %slice.19), channel_id=1, source_target_pairs={{0,4},{1,3},{2,6},{3,1},{4,0},{5,7},{6,2},{7,5},{8,12},{9,11},{10,... | collective-permute-start | bytes 786440 | tf_op jit(solution)/shard_map/ppermute | solution.py:41
  55.9 3.1 %collective-permute-done.15 = f32[32,2048]{1,0:T(8,128)} collective-permute-done((f32[32,2048]{1,0:T(8,128)}, f32[32,2048]{1,0:T(8,128)}, u32[]{:S(2)}, u32[]{:S(2)}) %collective-permute-start.15) | collective-permute-done | bytes 262176 | tf_op jit(solution)/shard_map/ppermute | solution.py:41
  60.0 2.1 %collective-permute-start.16 = (bf16[32,2048]{1,0:T(8,128)(2,1)S(1)}, bf16[32,2048]{1,0:T(8,128)(2,1)S(1)}, u32[]{:S(2)}, u32[]{:S(2)}) collective-permute-start(bf16[32,2048]{1,0:T(8,128)(2,1)S(1)} %fusion.6), channel_id=1, source_target_pairs={{0,4},{1,3},{2,6},{3,1},{4,0},{5,7},{6,2},{7,5},{8,12},{9,11},{10,... | collective-permute-start | bytes 393224 | tf_op jit(solution)/shard_map/ppermute | solution.py:41
  64.1 5.0 %pack_grads.1.rows_ref = bf16[256,7168]{1,0:T(8,128)(2,1)S(1)} custom-call(bf16[256,384]{1,0:T(8,128)(2,1)S(1)} %fusion.3.onehot_ref, bf16[48,7168]{1,0:T(8,128)(2,1)} %bitcast.11, bf16[48,7168]{1,0:T(8,128)(2,1)} %copy-done.2, bf16[48,7168]{1,0:T(8,128)(2,1)} %copy-done.3, bf16[48,7168]{1,0:T(8,128)(2,1)} %copy-done.4, ...), custom_call_target="tpu_custom_call" | custom-call | flops 1409286144 | bytes 9175040 | tf_op jit(solution)/shard_map/pack_grads/pallas_call | solution.py:145
  69.1 6.2 %rotate_grads.5 = (f32[256,1024]{1,0:T(8,128)S(1)}, bf16[256,1024]{1,0:T(8,128)(2,1)S(1)}) custom-call(bf16[256,7168]{1,0:T(8,128)(2,1)S(1)} %pack_grads.1.rows_ref, bf16[7168,3584]{1,0:T(8,128)(2,1)} %basis_ref.7), custom_call_target="tpu_custom_call" | custom-call | flops 3758096384 | bytes 19922944 | tf_op jit(solution)/shard_map/rotate_grads/pallas_call | solution.py:198
  75.4 3.9 %rotate_grads.7 = (f32[256,512]{1,0:T(8,128)S(1)}, bf16[256,512]{1,0:T(8,128)(2,1)S(1)}) custom-call(bf16[256,7168]{1,0:T(8,128)(2,1)S(1)} %pack_grads.1.rows_ref, bf16[7168,3584]{1,0:T(8,128)(2,1)} %basis_ref.7), custom_call_target="tpu_custom_call" | custom-call | flops 1879048192 | bytes 11796480 | tf_op jit(solution)/shard_map/rotate_grads/pallas_call | solution.py:198
  79.2 5.3 %collective-permute-start.25 = (bf16[256,512]{1,0:T(8,128)(2,1)S(1)}, bf16[256,512]{1,0:T(8,128)(2,1)S(1)}, u32[]{:S(2)}, u32[]{:S(2)}) collective-permute-start(bf16[256,512]{1,0:T(8,128)(2,1)S(1)} %get-tuple-element.24), channel_id=1, source_target_pairs={{0,8},{24,16},{1,9},{25,17},{2,10},{26,18},{3,11},{27,19},{4,12},{... | collective-permute-start | bytes 786440 | tf_op jit(solution)/shard_map/ppermute | solution.py:405
  84.6 6.2 %rotate_grads.4 = (f32[256,1024]{1,0:T(8,128)S(1)}, bf16[256,1024]{1,0:T(8,128)(2,1)S(1)}) custom-call(bf16[256,7168]{1,0:T(8,128)(2,1)S(1)} %pack_grads.1.rows_ref, bf16[7168,3584]{1,0:T(8,128)(2,1)} %basis_ref.7), custom_call_target="tpu_custom_call" | custom-call | flops 3758096384 | bytes 19922944 | tf_op jit(solution)/shard_map/rotate_grads/pallas_call | solution.py:198
  92.4 1.6 collective-permute-start.17
  94.7 6.2 %rotate_grads.6 = (f32[256,1024]{1,0:T(8,128)S(1)}, bf16[256,1024]{1,0:T(8,128)(2,1)S(1)}) custom-call(bf16[256,7168]{1,0:T(8,128)(2,1)S(1)} %pack_grads.1.rows_ref, bf16[7168,3584]{1,0:T(8,128)(2,1)} %basis_ref.7), custom_call_target="tpu_custom_call" | custom-call | flops 3758096384 | bytes 19922944 | tf_op jit(solution)/shard_map/rotate_grads/pallas_call | solution.py:198
  100.9 4.1 %collective-permute-start.7 = (bf16[256,1024]{1,0:T(8,128)(2,1)S(1)}, bf16[256,1024]{1,0:T(8,128)(2,1)S(1)}, u32[]{:S(2)}, u32[]{:S(2)}) collective-permute-start(bf16[256,1024]{1,0:T(8,128)(2,1)S(1)} %get-tuple-element.16), channel_id=1, source_target_pairs={{0,8},{24,16},{1,9},{25,17},{2,10},{26,18},{3,11},{27,19},{4,12},{... | collective-permute-start | bytes 1572872 | tf_op jit(solution)/shard_map/ppermute | solution.py:405
  108.8 8.5 %collective-permute-done.7 = bf16[256,1024]{1,0:T(8,128)(2,1)S(1)} collective-permute-done((bf16[256,1024]{1,0:T(8,128)(2,1)S(1)}, bf16[256,1024]{1,0:T(8,128)(2,1)S(1)}, u32[]{:S(2)}, u32[]{:S(2)}) %collective-permute-start.7) | collective-permute-done | bytes 524320 | tf_op jit(solution)/shard_map/ppermute | solution.py:405
  118.1 8.0 %collective-permute-done.22 = bf16[256,1024]{1,0:T(8,128)(2,1)S(1)} collective-permute-done((bf16[256,1024]{1,0:T(8,128)(2,1)S(1)}, bf16[256,1024]{1,0:T(8,128)(2,1)S(1)}, u32[]{:S(2)}, u32[]{:S(2)}) %collective-permute-start.22) | collective-permute-done | bytes 524320 | tf_op jit(solution)/shard_map/ppermute | solution.py:405
  127.2 3.1 %project.7.projected_ref = f32[2,256,512]{2,1,0:T(8,128)S(1)} custom-call(bf16[256,2048]{1,0:T(8,128)(2,1)S(1)} %pad_maximum_fusion.acts_ref, bf16[2,3584,2048]{2,1,0:T(8,128)(2,1)} %queries_ref.7), custom_call_target="tpu_custom_call" | custom-call | flops 1073741824 | bytes 5242880 | tf_op jit(solution)/shard_map/project/pallas_call | solution.py:296
  133.8 1.5 collective-permute-start.24
  135.3 4.6 %project.5.projected_ref = f32[2,256,1024]{2,1,0:T(8,128)S(1)} custom-call(bf16[256,2048]{1,0:T(8,128)(2,1)S(1)} %pad_maximum_fusion.acts_ref, bf16[2,3584,2048]{2,1,0:T(8,128)(2,1)} %queries_ref.7), custom_call_target="tpu_custom_call" | custom-call | flops 2147483648 | bytes 10485760 | tf_op jit(solution)/shard_map/project/pallas_call | solution.py:296
  139.9 4.6 %project.4.projected_ref = f32[2,256,1024]{2,1,0:T(8,128)S(1)} custom-call(bf16[256,2048]{1,0:T(8,128)(2,1)S(1)} %pad_maximum_fusion.acts_ref, bf16[2,3584,2048]{2,1,0:T(8,128)(2,1)} %queries_ref.7), custom_call_target="tpu_custom_call" | custom-call | flops 2147483648 | bytes 10485760 | tf_op jit(solution)/shard_map/project/pallas_call | solution.py:296
  144.5 4.6 %project.6.projected_ref = f32[2,256,1024]{2,1,0:T(8,128)S(1)} custom-call(bf16[256,2048]{1,0:T(8,128)(2,1)S(1)} %pad_maximum_fusion.acts_ref, bf16[2,3584,2048]{2,1,0:T(8,128)(2,1)} %queries_ref.7), custom_call_target="tpu_custom_call" | custom-call | flops 2147483648 | bytes 10485760 | tf_op jit(solution)/shard_map/project/pallas_call | solution.py:296
  149.4 10.7 %collective-permute-done.9.outward_ref = bf16[256,1024]{1,0:T(8,128)(2,1)S(1)} collective-permute-done((bf16[256,1024]{1,0:T(8,128)(2,1)S(1)}, bf16[256,1024]{1,0:T(8,128)(2,1)S(1)}, u32[]{:S(2)}, u32[]{:S(2)}) %collective-permute-start.9) | collective-permute-done | bytes 524320 | tf_op jit(solution)/shard_map/ppermute | solution.py:418
  160.3 7.8 %collective-permute-done.24.outward_ref = bf16[256,1024]{1,0:T(8,128)(2,1)S(1)} collective-permute-done((bf16[256,1024]{1,0:T(8,128)(2,1)S(1)}, bf16[256,1024]{1,0:T(8,128)(2,1)S(1)}, u32[]{:S(2)}, u32[]{:S(2)}) %collective-permute-start.24) | collective-permute-done | bytes 524320 | tf_op jit(solution)/shard_map/ppermute | solution.py:418
  168.9 11.2 %all_to_all.9 = f32[32,1,16]{2,1,0:T(1,128)S(1)} all-to-all(f32[32,1,16]{2,1,0:T(1,128)S(1)} %reshape.101), channel_id=1, replica_groups=mesh['row'=4,'col'=8] {'row','col'}, dimensions={0} | all-to-all | bytes 4096 | tf_op jit(solution)/shard_map/all_to_all | solution.py:428
  (93 shorter events, 23.5 us)
Async XLA Ops:
  0.0 11.6 %collective-permute-start.10 = (bf16[96,1024]{1,0:T(8,128)(2,1)}, bf16[96,1024]{1,0:T(8,128)(2,1)S(1)}, u32[]{:S(2)}, u32[]{:S(2)}) collective-permute-start(bf16[96,1024]{1,0:T(8,128)(2,1)} %bitcast.7), channel_id=1, source_target_pairs={{0,8},{8,0},{16,24},{24,16},{1,9},{9,1},{17,25},{25,17},{2,10},{10... | collective-permute-start | bytes 589832 | tf_op jit(solution)/shard_map/ppermute | solution.py:378
  3.1 17.3 %collective-permute-start.11 = (bf16[96,1024]{1,0:T(8,128)(2,1)}, bf16[96,1024]{1,0:T(8,128)(2,1)S(1)}, u32[]{:S(2)}, u32[]{:S(2)}) collective-permute-start(bf16[96,1024]{1,0:T(8,128)(2,1)} %bitcast.8), channel_id=1, source_target_pairs={{0,16},{8,24},{16,0},{24,8},{1,17},{9,25},{17,1},{25,9},{2,18},{10... | collective-permute-start | bytes 589832 | tf_op jit(solution)/shard_map/ppermute | solution.py:378
  5.6 14.7 %collective-permute-start.12 = (bf16[96,1024]{1,0:T(8,128)(2,1)}, bf16[96,1024]{1,0:T(8,128)(2,1)S(1)}, u32[]{:S(2)}, u32[]{:S(2)}) collective-permute-start(bf16[96,1024]{1,0:T(8,128)(2,1)} %bitcast.9), channel_id=1, source_target_pairs={{0,24},{8,16},{16,8},{24,0},{1,25},{9,17},{17,9},{25,1},{2,26},{10... | collective-permute-start | bytes 589832 | tf_op jit(solution)/shard_map/ppermute | solution.py:378
  21.3 3.3 %copy-start.1 = (bf16[1,48,7168]{2,1,0:T(8,128)(2,1)S(1)}, bf16[1,48,7168]{2,1,0:T(8,128)(2,1)}, u32[]{:S(2)}) copy-start(bf16[1,48,7168]{2,1,0:T(8,128)(2,1)} %param.6) | copy-start | bytes 2064388
  24.5 2.7 %collective-permute-start.13 = (f32[128,2048]{1,0:T(8,128)S(1)}, f32[128,2048]{1,0:T(8,128)S(1)}, u32[]{:S(2)}, u32[]{:S(2)}) collective-permute-start(f32[128,2048]{1,0:T(8,128)S(1)} %get-tuple-element.18), channel_id=1, source_target_pairs={{0,1},{1,0},{2,3},{3,2},{4,5},{5,4},{6,7},{7,6},{8,9},{9,8},{10,11... | collective-permute-start | bytes 3145736 | tf_op jit(solution)/shard_map/ppermute | solution.py:35
  24.6 15.2 %collective-permute-start = (bf16[48,7168]{1,0:T(8,128)(2,1)S(1)}, bf16[48,7168]{1,0:T(8,128)(2,1)S(1)}, u32[]{:S(2)}, u32[]{:S(2)}) collective-permute-start(bf16[48,7168]{1,0:T(8,128)(2,1)S(1)} %bitcast.12), channel_id=1, source_target_pairs={{0,2},{1,5},{2,0},{3,7},{4,6},{5,1},{6,4},{7,3},{8,10},{9,13},{10,... | collective-permute-start | bytes 2064392 | tf_op jit(solution)/shard_map/ppermute | solution.py:41
  27.4 23.6 %collective-permute-start.14 = (f32[64,2048]{1,0:T(8,128)S(1)}, f32[64,2048]{1,0:T(8,128)S(1)}, u32[]{:S(2)}, u32[]{:S(2)}) collective-permute-start(f32[64,2048]{1,0:T(8,128)S(1)} %slice.17), channel_id=1, source_target_pairs={{0,2},{1,5},{2,0},{3,7},{4,6},{5,1},{6,4},{7,3},{8,10},{9,13},{10,... | collective-permute-start | bytes 1572872 | tf_op jit(solution)/shard_map/ppermute | solution.py:41
  29.0 26.1 %collective-permute-start.1 = (bf16[48,7168]{1,0:T(8,128)(2,1)S(1)}, bf16[48,7168]{1,0:T(8,128)(2,1)S(1)}, u32[]{:S(2)}, u32[]{:S(2)}) collective-permute-start(bf16[48,7168]{1,0:T(8,128)(2,1)S(1)} %bitcast.13), channel_id=1, source_target_pairs={{0,4},{1,3},{2,6},{3,1},{4,0},{5,7},{6,2},{7,5},{8,12},{9,11},{10,... | collective-permute-start | bytes 2064392 | tf_op jit(solution)/shard_map/ppermute | solution.py:41
  39.8 22.4 %copy-start.2 = (bf16[48,7168]{1,0:T(8,128)(2,1)}, bf16[48,7168]{1,0:T(8,128)(2,1)S(1)}, u32[]{:S(2)}) copy-start(bf16[48,7168]{1,0:T(8,128)(2,1)S(1)} %collective-permute-done.refs_1_) | copy-start | bytes 2064388
  39.8 15.7 %collective-permute-start.2 = (bf16[48,7168]{1,0:T(8,128)(2,1)S(1)}, bf16[48,7168]{1,0:T(8,128)(2,1)S(1)}, u32[]{:S(2)}, u32[]{:S(2)}) collective-permute-start(bf16[48,7168]{1,0:T(8,128)(2,1)S(1)} %collective-permute-done.refs_1_), channel_id=1, source_target_pairs={{0,4},{1,3},{2,6},{3,1},{4,0},{5,7},{6,2},{7,5},{8,12},{9,11},{10,... | collective-permute-start | bytes 2064392 | tf_op jit(solution)/shard_map/ppermute | solution.py:41
  51.9 7.2 %collective-permute-start.15 = (f32[32,2048]{1,0:T(8,128)}, f32[32,2048]{1,0:T(8,128)}, u32[]{:S(2)}, u32[]{:S(2)}) collective-permute-start(f32[32,2048]{1,0:T(8,128)} %slice.19), channel_id=1, source_target_pairs={{0,4},{1,3},{2,6},{3,1},{4,0},{5,7},{6,2},{7,5},{8,12},{9,11},{10,... | collective-permute-start | bytes 786440 | tf_op jit(solution)/shard_map/ppermute | solution.py:41
  54.4 7.7 %collective-permute-start.3 = (bf16[48,7168]{1,0:T(8,128)(2,1)S(1)}, bf16[48,7168]{1,0:T(8,128)(2,1)}, u32[]{:S(2)}, u32[]{:S(2)}) collective-permute-start(bf16[48,7168]{1,0:T(8,128)(2,1)S(1)} %bitcast.14), channel_id=1, source_target_pairs={{0,1},{1,0},{2,3},{3,2},{4,5},{5,4},{6,7},{7,6},{8,9},{9,8},{10,11... | collective-permute-start | bytes 2064392 | tf_op jit(solution)/shard_map/ppermute | solution.py:35
  54.5 7.6 %collective-permute-start.4 = (bf16[48,7168]{1,0:T(8,128)(2,1)S(1)}, bf16[48,7168]{1,0:T(8,128)(2,1)S(1)}, u32[]{:S(2)}, u32[]{:S(2)}) collective-permute-start(bf16[48,7168]{1,0:T(8,128)(2,1)S(1)} %collective-permute-done.refs_1_), channel_id=1, source_target_pairs={{0,1},{1,0},{2,3},{3,2},{4,5},{5,4},{6,7},{7,6},{8,9},{9,8},{10,11... | collective-permute-start | bytes 2064392 | tf_op jit(solution)/shard_map/ppermute | solution.py:35
  55.1 7.1 %copy-start.3 = (bf16[48,7168]{1,0:T(8,128)(2,1)}, bf16[48,7168]{1,0:T(8,128)(2,1)S(1)}, u32[]{:S(2)}) copy-start(bf16[48,7168]{1,0:T(8,128)(2,1)S(1)} %collective-permute-done.1.refs_2_) | copy-start | bytes 2064388
  55.1 7.1 %collective-permute-start.5 = (bf16[48,7168]{1,0:T(8,128)(2,1)S(1)}, bf16[48,7168]{1,0:T(8,128)(2,1)S(1)}, u32[]{:S(2)}, u32[]{:S(2)}) collective-permute-start(bf16[48,7168]{1,0:T(8,128)(2,1)S(1)} %collective-permute-done.1.refs_2_), channel_id=1, source_target_pairs={{0,1},{1,0},{2,3},{3,2},{4,5},{5,4},{6,7},{7,6},{8,9},{9,8},{10,11... | collective-permute-start | bytes 2064392 | tf_op jit(solution)/shard_map/ppermute | solution.py:35
  55.5 6.7 %copy-start.4 = (bf16[48,7168]{1,0:T(8,128)(2,1)}, bf16[48,7168]{1,0:T(8,128)(2,1)S(1)}, u32[]{:S(2)}) copy-start(bf16[48,7168]{1,0:T(8,128)(2,1)S(1)} %collective-permute-done.2.refs_3_) | copy-start | bytes 2064388
  55.5 6.7 %collective-permute-start.6 = (bf16[48,7168]{1,0:T(8,128)(2,1)S(1)}, bf16[48,7168]{1,0:T(8,128)(2,1)S(1)}, u32[]{:S(2)}, u32[]{:S(2)}) collective-permute-start(bf16[48,7168]{1,0:T(8,128)(2,1)S(1)} %collective-permute-done.2.refs_3_), channel_id=1, source_target_pairs={{0,1},{1,0},{2,3},{3,2},{4,5},{5,4},{6,7},{7,6},{8,9},{9,8},{10,11... | collective-permute-start | bytes 2064392 | tf_op jit(solution)/shard_map/ppermute | solution.py:35
  60.0 32.3 %collective-permute-start.16 = (bf16[32,2048]{1,0:T(8,128)(2,1)S(1)}, bf16[32,2048]{1,0:T(8,128)(2,1)S(1)}, u32[]{:S(2)}, u32[]{:S(2)}) collective-permute-start(bf16[32,2048]{1,0:T(8,128)(2,1)S(1)} %fusion.6), channel_id=1, source_target_pairs={{0,4},{1,3},{2,6},{3,1},{4,0},{5,7},{6,2},{7,5},{8,12},{9,11},{10,... | collective-permute-start | bytes 393224 | tf_op jit(solution)/shard_map/ppermute | solution.py:41
  79.2 14.7 %collective-permute-start.25 = (bf16[256,512]{1,0:T(8,128)(2,1)S(1)}, bf16[256,512]{1,0:T(8,128)(2,1)S(1)}, u32[]{:S(2)}, u32[]{:S(2)}) collective-permute-start(bf16[256,512]{1,0:T(8,128)(2,1)S(1)} %get-tuple-element.24), channel_id=1, source_target_pairs={{0,8},{24,16},{1,9},{25,17},{2,10},{26,18},{3,11},{27,19},{4,12},{... | collective-permute-start | bytes 786440 | tf_op jit(solution)/shard_map/ppermute | solution.py:405
  90.8 17.1 %collective-permute-start.19 = (bf16[256,1024]{1,0:T(8,128)(2,1)S(1)}, bf16[256,1024]{1,0:T(8,128)(2,1)S(1)}, u32[]{:S(2)}, u32[]{:S(2)}) collective-permute-start(bf16[256,1024]{1,0:T(8,128)(2,1)S(1)} %get-tuple-element.20), channel_id=1, source_target_pairs={{0,8},{24,16},{1,9},{25,17},{2,10},{26,18},{3,11},{27,19},{4,12},{... | collective-permute-start | bytes 1572872 | tf_op jit(solution)/shard_map/ppermute | solution.py:405
  92.4 14.0 %collective-permute-start.17 = (bf16[64,2048]{1,0:T(8,128)(2,1)S(1)}, bf16[64,2048]{1,0:T(8,128)(2,1)S(1)}, u32[]{:S(2)}, u32[]{:S(2)}) collective-permute-start(bf16[64,2048]{1,0:T(8,128)(2,1)S(1)} %pad_maximum_fusion.2), channel_id=1, source_target_pairs={{0,2},{1,5},{2,0},{3,7},{4,6},{5,1},{6,4},{7,3},{8,10},{9,13},{10,... | collective-permute-start | bytes 786440 | tf_op jit(solution)/shard_map/ppermute | solution.py:41
  94.0 12.5 %collective-permute-start.26 = (bf16[256,512]{1,0:T(8,128)(2,1)S(1)}, bf16[256,512]{1,0:T(8,128)(2,1)S(1)}, u32[]{:S(2)}, u32[]{:S(2)}) collective-permute-start(bf16[256,512]{1,0:T(8,128)(2,1)S(1)} %fusion.5), channel_id=1, source_target_pairs={{8,16},{16,8},{9,17},{17,9},{10,18},{18,10},{11,19},{19,11},{12,20... | collective-permute-start | bytes 786440 | tf_op jit(solution)/shard_map/ppermute | solution.py:405
  100.9 16.3 %collective-permute-start.7 = (bf16[256,1024]{1,0:T(8,128)(2,1)S(1)}, bf16[256,1024]{1,0:T(8,128)(2,1)S(1)}, u32[]{:S(2)}, u32[]{:S(2)}) collective-permute-start(bf16[256,1024]{1,0:T(8,128)(2,1)S(1)} %get-tuple-element.16), channel_id=1, source_target_pairs={{0,8},{24,16},{1,9},{25,17},{2,10},{26,18},{3,11},{27,19},{4,12},{... | collective-permute-start | bytes 1572872 | tf_op jit(solution)/shard_map/ppermute | solution.py:405
  105.0 21.2 %collective-permute-start.22 = (bf16[256,1024]{1,0:T(8,128)(2,1)S(1)}, bf16[256,1024]{1,0:T(8,128)(2,1)S(1)}, u32[]{:S(2)}, u32[]{:S(2)}) collective-permute-start(bf16[256,1024]{1,0:T(8,128)(2,1)S(1)} %get-tuple-element.22), channel_id=1, source_target_pairs={{0,8},{24,16},{1,9},{25,17},{2,10},{26,18},{3,11},{27,19},{4,12},{... | collective-permute-start | bytes 1572872 | tf_op jit(solution)/shard_map/ppermute | solution.py:405
  106.4 20.6 %collective-permute-start.18 = (bf16[128,2048]{1,0:T(8,128)(2,1)S(1)}, bf16[128,2048]{1,0:T(8,128)(2,1)S(1)}, u32[]{:S(2)}, u32[]{:S(2)}) collective-permute-start(bf16[128,2048]{1,0:T(8,128)(2,1)S(1)} %pad_maximum_fusion.1), channel_id=1, source_target_pairs={{0,1},{1,0},{2,3},{3,2},{4,5},{5,4},{6,7},{7,6},{8,9},{9,8},{10,11... | collective-permute-start | bytes 1572872 | tf_op jit(solution)/shard_map/ppermute | solution.py:35
  106.6 23.6 %collective-permute-start.27 = (bf16[256,512]{1,0:T(8,128)(2,1)S(1)}, bf16[256,512]{1,0:T(8,128)(2,1)S(1)}, u32[]{:S(2)}, u32[]{:S(2)}) collective-permute-start(bf16[256,512]{1,0:T(8,128)(2,1)S(1)} %add_convert_fusion.3.kept_ref), channel_id=1, source_target_pairs={{8,0},{16,24},{9,1},{17,25},{10,2},{18,26},{11,3},{19,27},{12,4},{... | collective-permute-start | bytes 786440 | tf_op jit(solution)/shard_map/ppermute | solution.py:418
  108.1 22.3 %collective-permute-start.20 = (bf16[256,1024]{1,0:T(8,128)(2,1)S(1)}, bf16[256,1024]{1,0:T(8,128)(2,1)S(1)}, u32[]{:S(2)}, u32[]{:S(2)}) collective-permute-start(bf16[256,1024]{1,0:T(8,128)(2,1)S(1)} %fusion.1), channel_id=1, source_target_pairs={{8,16},{16,8},{9,17},{17,9},{10,18},{18,10},{11,19},{19,11},{12,20... | collective-permute-start | bytes 1572872 | tf_op jit(solution)/shard_map/ppermute | solution.py:405
  117.4 14.5 %collective-permute-start.8 = (bf16[256,1024]{1,0:T(8,128)(2,1)S(1)}, bf16[256,1024]{1,0:T(8,128)(2,1)S(1)}, u32[]{:S(2)}, u32[]{:S(2)}) collective-permute-start(bf16[256,1024]{1,0:T(8,128)(2,1)S(1)} %fusion), channel_id=1, source_target_pairs={{8,16},{16,8},{9,17},{17,9},{10,18},{18,10},{11,19},{19,11},{12,20... | collective-permute-start | bytes 1572872 | tf_op jit(solution)/shard_map/ppermute | solution.py:405
  126.3 7.2 %collective-permute-start.23 = (bf16[256,1024]{1,0:T(8,128)(2,1)S(1)}, bf16[256,1024]{1,0:T(8,128)(2,1)S(1)}, u32[]{:S(2)}, u32[]{:S(2)}) collective-permute-start(bf16[256,1024]{1,0:T(8,128)(2,1)S(1)} %fusion.2), channel_id=1, source_target_pairs={{8,16},{16,8},{9,17},{17,9},{10,18},{18,10},{11,19},{19,11},{12,20... | collective-permute-start | bytes 1572872 | tf_op jit(solution)/shard_map/ppermute | solution.py:405
  130.7 18.5 %collective-permute-start.21 = (bf16[256,1024]{1,0:T(8,128)(2,1)S(1)}, bf16[256,1024]{1,0:T(8,128)(2,1)S(1)}, u32[]{:S(2)}, u32[]{:S(2)}) collective-permute-start(bf16[256,1024]{1,0:T(8,128)(2,1)S(1)} %add_convert_fusion.1.kept_ref), channel_id=1, source_target_pairs={{8,0},{16,24},{9,1},{17,25},{10,2},{18,26},{11,3},{19,27},{12,4},{... | collective-permute-start | bytes 1572872 | tf_op jit(solution)/shard_map/ppermute | solution.py:418
  132.2 27.9 %collective-permute-start.9 = (bf16[256,1024]{1,0:T(8,128)(2,1)S(1)}, bf16[256,1024]{1,0:T(8,128)(2,1)S(1)}, u32[]{:S(2)}, u32[]{:S(2)}) collective-permute-start(bf16[256,1024]{1,0:T(8,128)(2,1)S(1)} %add_convert_fusion.2.kept_ref), channel_id=1, source_target_pairs={{8,0},{16,24},{9,1},{17,25},{10,2},{18,26},{11,3},{19,27},{12,4},{... | collective-permute-start | bytes 1572872 | tf_op jit(solution)/shard_map/ppermute | solution.py:418
  133.8 34.3 %collective-permute-start.24 = (bf16[256,1024]{1,0:T(8,128)(2,1)S(1)}, bf16[256,1024]{1,0:T(8,128)(2,1)S(1)}, u32[]{:S(2)}, u32[]{:S(2)}) collective-permute-start(bf16[256,1024]{1,0:T(8,128)(2,1)S(1)} %add_convert_fusion.kept_ref), channel_id=1, source_target_pairs={{8,0},{16,24},{9,1},{17,25},{10,2},{18,26},{11,3},{19,27},{12,4},{... | collective-permute-start | bytes 1572872 | tf_op jit(solution)/shard_map/ppermute | solution.py:418
  (4 other events, 3.7 us)

commit v3 on v2

--- a/solution.py
+++ b/solution.py
@@ -131,10 +131,9 @@
                 fetch([r.at[:, columns] for r in sources], rows_ref.at[:, columns], sems.at[p])
             )
 
-        start(0)
         for p in range(parts):
-            if p + 1 < parts:
-                start(p + 1)
+            start(p)
+        for p in range(parts):
             for copy in copies[p]:
                 copy.wait()
             columns = pl.ds(p * width, width)
@@ -318,7 +317,9 @@
     count, tokens, width = projected.shape
     unit = block_of(width, WIDE)
 
-    def kernel(inner_ref, kept_ref, outward_ref, projected_ref, out_ref):
+    def kernel(inner_ref, kept_ref, *refs):
+        projected_ref, out_ref = refs[-2:]
+
         def add(total_ref):
             parts = [None] * count
             for at in range(0, width, unit):
@@ -332,11 +333,17 @@
                 out_ref[q] = parts[q]
 
         pl.when(inner_ref[0] == 1)(lambda: add(kept_ref))
-        pl.when(inner_ref[0] == 0)(lambda: add(outward_ref))
+
+        @pl.when(inner_ref[0] == 0)
+        def _():
+            if outward is None:
+                out_ref[...] = jnp.zeros_like(out_ref)
+            else:
+                add(refs[0])
 
     return pl.pallas_call(
         kernel,
-        in_specs=[pl.BlockSpec(memory_space=pltpu.SMEM)] + [VMEM] * 3,
+        in_specs=[pl.BlockSpec(memory_space=pltpu.SMEM)] + [VMEM] * (2 if outward is None else 3),
         out_specs=VMEM,
         out_shape=jax.ShapeDtypeStruct((count, tokens, LANES), F32),
         compiler_params=limit(tokens * (width * (4 * count + 4) + 8 * count * LANES + 8 * unit)),
@@ -346,7 +353,7 @@
             transcendentals=0,
         ),
         name="score",
-    )(inner, kept, outward, projected)
+    )(inner, kept, *([] if outward is None else [outward]), projected)
 
 
 def line_steps(count):
@@ -410,15 +417,22 @@
 
     z = lax.axis_index("row")
     inner = ((z == rows // 2 - 1) | (z == rows // 2)).astype(jnp.int32).reshape(1)
+    last = len(chunks) - 1
     scores = 0.0
-    for start, width, sent in chunks:
+    for k, (start, width, sent) in enumerate(chunks):
         projected = project(rot_acts, queries, start, width)
         kept = back = sent
-        for step, pairs in enumerate(outward):
-            got = lax.ppermute(sent, "row", pairs)
-            taken = (z == pairs[0][1]) | (z == pairs[1][1])
-            back = got if step == 0 else jnp.where(taken, got, back)
-            sent = back
+        if k == last:
+            for pairs in inward[:-1]:
+                got = lax.ppermute(projected.astype(BF16), "row", pairs)
+                projected = projected + got.astype(F32)
+            back = None
+        else:
+            for step, pairs in enumerate(outward):
+                got = lax.ppermute(sent, "row", pairs)
+                taken = (z == pairs[0][1]) | (z == pairs[1][1])
+                back = got if step == 0 else jnp.where(taken, got, back)
+                sent = back
         scores = scores + score(inner, kept, back, projected)
 
     count = scores.shape[0]

time: 181 us -> 189 us (1.044)
  starting transfers between devices: 40.6 us -> 45.4 us
  waiting for transfers between devices: 69.4 us -> 73.2 us
    ppermute x0 -> x1, starting transfers between devices: none -> 6.11 us  [program(): got = lax.ppermute(projected.astype(BF16), 'row', pairs)]
    ppermute x4 -> x3, waiting for transfers between devices: 18.5 us -> 20.9 us  [program(): got = lax.ppermute(sent, 'row', pairs)]
    ppermute x4 -> x3, starting transfers between devices: 5.39 us -> 4.1 us  [program(): got = lax.ppermute(sent, 'row', pairs)]
  transfers between devices with their start and end apart: 28 -> 28, of which waited for: 11 -> 12; matrix products, arithmetic and copies ran while one was open for 4% -> 4% of each run, Pallas kernels for 25% -> 24%
where the time goes in v3:
time: 189 us
  waiting for transfers between devices  73.2 us (39%)
  Pallas kernels  47.9 us (25%)
  starting transfers between devices  45.4 us (24%)
  blocking collectives  11.1 us (6%)
  other arithmetic  5.94 us (3%)
  local copies, waits for them, and re-layouts  4.85 us (3%)
    pallas_call x4, Pallas kernels, rotate_grads(): pl.pallas_call(kernel, in_specs=[VMEM, HBM], out_specs=[VMEM, VMEM], out_...  22.6 us
    ppermute x7, waiting for transfers between devices, far(): lax.ppermute(value, self.axis, [(i, partner(i)) for i in range(self.count)])  21.4 us
    ppermute x3, waiting for transfers between devices, program(): got = lax.ppermute(sent, 'row', pairs)  20.9 us
    ppermute x8, waiting for transfers between devices, program(): total = total + lax.ppermute(sent, 'row', pairs).astype(F32)  17.9 us
    pallas_call x4, Pallas kernels, project(): pl.pallas_call(kernel, in_specs=[VMEM, HBM], out_specs=VMEM, out_shape=ja...  16.9 us
    ppermute x8, starting transfers between devices, program(): total = total + lax.ppermute(sent, 'row', pairs).astype(F32)  15 us
    ppermute x7, starting transfers between devices, far(): lax.ppermute(value, self.axis, [(i, partner(i)) for i in range(self.count)])  13.4 us
    ppermute x3, waiting for transfers between devices, program(): lax.ppermute(held[0], 'row', [(i, i ^ apart) for i in range(rows)])  11.9 us
  transfers between devices with their start and end apart: 28, of which 12 were waited for; matrix products, arithmetic and copies ran while one was open for 4% of the time, Pallas kernels for 24%

profile of v3, /device:TPU:0, one launch (start us, length us, event | category | flops | bytes accessed | tf_op | source)
XLA Modules:
  0.0 189.0 jit_solution(1973588439127709119)
XLA Ops:
  0.0 3.1 %collective-permute-start.10 = (bf16[96,1024]{1,0:T(8,128)(2,1)}, bf16[96,1024]{1,0:T(8,128)(2,1)S(1)}, u32[]{:S(2)}, u32[]{:S(2)}) collective-permute-start(bf16[96,1024]{1,0:T(8,128)(2,1)} %bitcast.7), channel_id=1, source_target_pairs={{0,8},{8,0},{16,24},{24,16},{1,9},{9,1},{17,25},{25,17},{2,10},{10... | collective-permute-start | bytes 589832 | tf_op jit(solution)/shard_map/ppermute | solution.py:385
  3.1 2.6 %collective-permute-start.11 = (bf16[96,1024]{1,0:T(8,128)(2,1)}, bf16[96,1024]{1,0:T(8,128)(2,1)S(1)}, u32[]{:S(2)}, u32[]{:S(2)}) collective-permute-start(bf16[96,1024]{1,0:T(8,128)(2,1)} %bitcast.8), channel_id=1, source_target_pairs={{0,16},{8,24},{16,0},{24,8},{1,17},{9,25},{17,1},{25,9},{2,18},{10... | collective-permute-start | bytes 589832 | tf_op jit(solution)/shard_map/ppermute | solution.py:385
  8.5 3.1 %collective-permute-done.10.refs_1_ = bf16[96,1024]{1,0:T(8,128)(2,1)S(1)} collective-permute-done((bf16[96,1024]{1,0:T(8,128)(2,1)}, bf16[96,1024]{1,0:T(8,128)(2,1)S(1)}, u32[]{:S(2)}, u32[]{:S(2)}) %collective-permute-start.10) | collective-permute-done | bytes 196640 | tf_op jit(solution)/shard_map/ppermute | solution.py:385
  11.6 8.7 %collective-permute-done.11.refs_2_ = bf16[96,1024]{1,0:T(8,128)(2,1)S(1)} collective-permute-done((bf16[96,1024]{1,0:T(8,128)(2,1)}, bf16[96,1024]{1,0:T(8,128)(2,1)S(1)}, u32[]{:S(2)}, u32[]{:S(2)}) %collective-permute-start.11) | collective-permute-done | bytes 196640 | tf_op jit(solution)/shard_map/ppermute | solution.py:385
  21.3 3.2 %rotate_acts.1 = (f32[128,2048]{1,0:T(8,128)S(1)}, f32[128,2048]{1,0:T(8,128)S(1)}) custom-call(bf16[256,384]{1,0:T(8,128)(2,1)S(1)} %fusion.4.onehot_ref, bf16[96,1024]{1,0:T(8,128)(2,1)S(1)} %bitcast.10, bf16[96,1024]{1,0:T(8,128)(2,1)S(1)} %collective-permute-done.10.refs_1_, bf16[96,1024]{1,0:T(8,128)(2,1)S(1)} %collective-permute-done.11.refs_2_, ...), custom_call_target="tpu_custom_call" | custom-call | flops 1275068416 | bytes 7077888 | tf_op jit(solution)/shard_map/rotate_acts/pallas_call | solution.py:245
  24.6 1.6 collective-permute-start
  27.4 1.6 collective-permute-start.14
  30.5 9.3 %collective-permute-done.refs_1_ = bf16[48,7168]{1,0:T(8,128)(2,1)S(1)} collective-permute-done((bf16[48,7168]{1,0:T(8,128)(2,1)S(1)}, bf16[48,7168]{1,0:T(8,128)(2,1)S(1)}, u32[]{:S(2)}, u32[]{:S(2)}) %collective-permute-start) | collective-permute-done | bytes 688160 | tf_op jit(solution)/shard_map/ppermute | solution.py:41
  39.8 2.5 %collective-permute-start.2 = (bf16[48,7168]{1,0:T(8,128)(2,1)S(1)}, bf16[48,7168]{1,0:T(8,128)(2,1)S(1)}, u32[]{:S(2)}, u32[]{:S(2)}) collective-permute-start(bf16[48,7168]{1,0:T(8,128)(2,1)S(1)} %collective-permute-done.refs_1_), channel_id=1, source_target_pairs={{0,4},{1,3},{2,6},{3,1},{4,0},{5,7},{6,2},{7,5},{8,12},{9,11},{10,... | collective-permute-start | bytes 2064392 | tf_op jit(solution)/shard_map/ppermute | solution.py:41
  42.3 8.7 %collective-permute-done.14 = f32[64,2048]{1,0:T(8,128)S(1)} collective-permute-done((f32[64,2048]{1,0:T(8,128)S(1)}, f32[64,2048]{1,0:T(8,128)S(1)}, u32[]{:S(2)}, u32[]{:S(2)}) %collective-permute-start.14) | collective-permute-done | bytes 524320 | tf_op jit(solution)/shard_map/ppermute | solution.py:41
  51.9 2.5 %collective-permute-start.15 = (f32[32,2048]{1,0:T(8,128)}, f32[32,2048]{1,0:T(8,128)}, u32[]{:S(2)}, u32[]{:S(2)}) collective-permute-start(f32[32,2048]{1,0:T(8,128)} %slice.19), channel_id=1, source_target_pairs={{0,4},{1,3},{2,6},{3,1},{4,0},{5,7},{6,2},{7,5},{8,12},{9,11},{10,... | collective-permute-start | bytes 786440 | tf_op jit(solution)/shard_map/ppermute | solution.py:41
  55.9 3.1 %collective-permute-done.15 = f32[32,2048]{1,0:T(8,128)} collective-permute-done((f32[32,2048]{1,0:T(8,128)}, f32[32,2048]{1,0:T(8,128)}, u32[]{:S(2)}, u32[]{:S(2)}) %collective-permute-start.15) | collective-permute-done | bytes 262176 | tf_op jit(solution)/shard_map/ppermute | solution.py:41
  60.0 2.1 %collective-permute-start.16 = (bf16[32,2048]{1,0:T(8,128)(2,1)S(1)}, bf16[32,2048]{1,0:T(8,128)(2,1)S(1)}, u32[]{:S(2)}, u32[]{:S(2)}) collective-permute-start(bf16[32,2048]{1,0:T(8,128)(2,1)S(1)} %fusion.6), channel_id=1, source_target_pairs={{0,4},{1,3},{2,6},{3,1},{4,0},{5,7},{6,2},{7,5},{8,12},{9,11},{10,... | collective-permute-start | bytes 393224 | tf_op jit(solution)/shard_map/ppermute | solution.py:41
  64.1 4.6 %pack_grads.1.rows_ref = bf16[256,7168]{1,0:T(8,128)(2,1)S(1)} custom-call(bf16[256,384]{1,0:T(8,128)(2,1)S(1)} %fusion.3.onehot_ref, bf16[48,7168]{1,0:T(8,128)(2,1)} %bitcast.11, bf16[48,7168]{1,0:T(8,128)(2,1)} %copy-done.2, bf16[48,7168]{1,0:T(8,128)(2,1)} %copy-done.3, bf16[48,7168]{1,0:T(8,128)(2,1)} %copy-done.4, ...), custom_call_target="tpu_custom_call" | custom-call | flops 1409286144 | bytes 9175040 | tf_op jit(solution)/shard_map/pack_grads/pallas_call | solution.py:144
  68.7 6.2 %rotate_grads.5 = (f32[256,1024]{1,0:T(8,128)S(1)}, bf16[256,1024]{1,0:T(8,128)(2,1)S(1)}) custom-call(bf16[256,7168]{1,0:T(8,128)(2,1)S(1)} %pack_grads.1.rows_ref, bf16[7168,3584]{1,0:T(8,128)(2,1)} %basis_ref.7), custom_call_target="tpu_custom_call" | custom-call | flops 3758096384 | bytes 19922944 | tf_op jit(solution)/shard_map/rotate_grads/pallas_call | solution.py:197
  74.9 3.9 %rotate_grads.7 = (f32[256,512]{1,0:T(8,128)S(1)}, bf16[256,512]{1,0:T(8,128)(2,1)S(1)}) custom-call(bf16[256,7168]{1,0:T(8,128)(2,1)S(1)} %pack_grads.1.rows_ref, bf16[7168,3584]{1,0:T(8,128)(2,1)} %basis_ref.7), custom_call_target="tpu_custom_call" | custom-call | flops 1879048192 | bytes 11796480 | tf_op jit(solution)/shard_map/rotate_grads/pallas_call | solution.py:197
  78.8 5.3 %collective-permute-start.25 = (bf16[256,512]{1,0:T(8,128)(2,1)S(1)}, bf16[256,512]{1,0:T(8,128)(2,1)S(1)}, u32[]{:S(2)}, u32[]{:S(2)}) collective-permute-start(bf16[256,512]{1,0:T(8,128)(2,1)S(1)} %get-tuple-element.24), channel_id=1, source_target_pairs={{0,8},{24,16},{1,9},{25,17},{2,10},{26,18},{3,11},{27,19},{4,12},{... | collective-permute-start | bytes 786440 | tf_op jit(solution)/shard_map/ppermute | solution.py:412
  84.2 6.2 %rotate_grads.4 = (f32[256,1024]{1,0:T(8,128)S(1)}, bf16[256,1024]{1,0:T(8,128)(2,1)S(1)}) custom-call(bf16[256,7168]{1,0:T(8,128)(2,1)S(1)} %pack_grads.1.rows_ref, bf16[7168,3584]{1,0:T(8,128)(2,1)} %basis_ref.7), custom_call_target="tpu_custom_call" | custom-call | flops 3758096384 | bytes 19922944 | tf_op jit(solution)/shard_map/rotate_grads/pallas_call | solution.py:197
  92.0 1.6 collective-permute-start.17
  94.3 6.2 %rotate_grads.6 = (f32[256,1024]{1,0:T(8,128)S(1)}, bf16[256,1024]{1,0:T(8,128)(2,1)S(1)}) custom-call(bf16[256,7168]{1,0:T(8,128)(2,1)S(1)} %pack_grads.1.rows_ref, bf16[7168,3584]{1,0:T(8,128)(2,1)} %basis_ref.7), custom_call_target="tpu_custom_call" | custom-call | flops 3758096384 | bytes 19922944 | tf_op jit(solution)/shard_map/rotate_grads/pallas_call | solution.py:197
  100.5 4.1 %collective-permute-start.7 = (bf16[256,1024]{1,0:T(8,128)(2,1)S(1)}, bf16[256,1024]{1,0:T(8,128)(2,1)S(1)}, u32[]{:S(2)}, u32[]{:S(2)}) collective-permute-start(bf16[256,1024]{1,0:T(8,128)(2,1)S(1)} %get-tuple-element.16), channel_id=1, source_target_pairs={{0,8},{24,16},{1,9},{25,17},{2,10},{26,18},{3,11},{27,19},{4,12},{... | collective-permute-start | bytes 1572872 | tf_op jit(solution)/shard_map/ppermute | solution.py:412
  107.0 9.8 %collective-permute-done.7 = bf16[256,1024]{1,0:T(8,128)(2,1)S(1)} collective-permute-done((bf16[256,1024]{1,0:T(8,128)(2,1)S(1)}, bf16[256,1024]{1,0:T(8,128)(2,1)S(1)}, u32[]{:S(2)}, u32[]{:S(2)}) %collective-permute-start.7) | collective-permute-done | bytes 524320 | tf_op jit(solution)/shard_map/ppermute | solution.py:412
  117.7 8.0 %collective-permute-done.22 = bf16[256,1024]{1,0:T(8,128)(2,1)S(1)} collective-permute-done((bf16[256,1024]{1,0:T(8,128)(2,1)S(1)}, bf16[256,1024]{1,0:T(8,128)(2,1)S(1)}, u32[]{:S(2)}, u32[]{:S(2)}) %collective-permute-start.22) | collective-permute-done | bytes 524320 | tf_op jit(solution)/shard_map/ppermute | solution.py:412
  126.7 3.1 %project.7 = f32[2,256,512]{2,1,0:T(8,128)S(1)} custom-call(bf16[256,2048]{1,0:T(8,128)(2,1)S(1)} %pad_maximum_fusion.acts_ref, bf16[2,3584,2048]{2,1,0:T(8,128)(2,1)} %queries_ref.7), custom_call_target="tpu_custom_call" | custom-call | flops 1073741824 | bytes 5242880 | tf_op jit(solution)/shard_map/project/pallas_call | solution.py:295
  129.9 6.1 %collective-permute-start.27 = (bf16[2,256,512]{2,1,0:T(8,128)(2,1)S(1)}, bf16[2,256,512]{2,1,0:T(8,128)(2,1)S(1)}, u32[]{:S(2)}, u32[]{:S(2)}) collective-permute-start(bf16[2,256,512]{2,1,0:T(8,128)(2,1)S(1)} %convert_element_type.88), channel_id=1, source_target_pairs={{0,8},{24,16},{1,9},{25,17},{2,10},{26,18},{3,11},{27,19},{4,12},{... | collective-permute-start | bytes 1572872 | tf_op jit(solution)/shard_map/ppermute | solution.py:427
  136.0 4.6 %project.5.refs_1_ = f32[2,256,1024]{2,1,0:T(8,128)S(1)} custom-call(bf16[256,2048]{1,0:T(8,128)(2,1)S(1)} %pad_maximum_fusion.acts_ref, bf16[2,3584,2048]{2,1,0:T(8,128)(2,1)} %queries_ref.7), custom_call_target="tpu_custom_call" | custom-call | flops 2147483648 | bytes 10485760 | tf_op jit(solution)/shard_map/project/pallas_call | solution.py:295
  145.5 4.6 %project.4.refs_1_ = f32[2,256,1024]{2,1,0:T(8,128)S(1)} custom-call(bf16[256,2048]{1,0:T(8,128)(2,1)S(1)} %pad_maximum_fusion.acts_ref, bf16[2,3584,2048]{2,1,0:T(8,128)(2,1)} %queries_ref.7), custom_call_target="tpu_custom_call" | custom-call | flops 2147483648 | bytes 10485760 | tf_op jit(solution)/shard_map/project/pallas_call | solution.py:295
  150.1 4.6 %project.6.refs_1_ = f32[2,256,1024]{2,1,0:T(8,128)S(1)} custom-call(bf16[256,2048]{1,0:T(8,128)(2,1)S(1)} %pad_maximum_fusion.acts_ref, bf16[2,3584,2048]{2,1,0:T(8,128)(2,1)} %queries_ref.7), custom_call_target="tpu_custom_call" | custom-call | flops 2147483648 | bytes 10485760 | tf_op jit(solution)/shard_map/project/pallas_call | solution.py:295
  154.9 2.6 %collective-permute-done.21.refs_0_ = bf16[256,1024]{1,0:T(8,128)(2,1)S(1)} collective-permute-done((bf16[256,1024]{1,0:T(8,128)(2,1)S(1)}, bf16[256,1024]{1,0:T(8,128)(2,1)S(1)}, u32[]{:S(2)}, u32[]{:S(2)}) %collective-permute-start.21) | collective-permute-done | bytes 524320 | tf_op jit(solution)/shard_map/ppermute | solution.py:432
  157.8 11.0 %collective-permute-done.9.refs_0_ = bf16[256,1024]{1,0:T(8,128)(2,1)S(1)} collective-permute-done((bf16[256,1024]{1,0:T(8,128)(2,1)S(1)}, bf16[256,1024]{1,0:T(8,128)(2,1)S(1)}, u32[]{:S(2)}, u32[]{:S(2)}) %collective-permute-start.9) | collective-permute-done | bytes 524320 | tf_op jit(solution)/shard_map/ppermute | solution.py:432
  169.0 7.3 %collective-permute-done.24.refs_0_ = bf16[256,1024]{1,0:T(8,128)(2,1)S(1)} collective-permute-done((bf16[256,1024]{1,0:T(8,128)(2,1)S(1)}, bf16[256,1024]{1,0:T(8,128)(2,1)S(1)}, u32[]{:S(2)}, u32[]{:S(2)}) %collective-permute-start.24) | collective-permute-done | bytes 524320 | tf_op jit(solution)/shard_map/ppermute | solution.py:432
  177.1 11.1 %all_to_all.9 = f32[32,1,16]{2,1,0:T(1,128)S(1)} all-to-all(f32[32,1,16]{2,1,0:T(1,128)S(1)} %reshape.101), channel_id=1, replica_groups=mesh['row'=4,'col'=8] {'row','col'}, dimensions={0} | all-to-all | bytes 4096 | tf_op jit(solution)/shard_map/all_to_all | solution.py:442
  (95 shorter events, 25.2 us)
Async XLA Ops:
  0.0 11.6 %collective-permute-start.10 = (bf16[96,1024]{1,0:T(8,128)(2,1)}, bf16[96,1024]{1,0:T(8,128)(2,1)S(1)}, u32[]{:S(2)}, u32[]{:S(2)}) collective-permute-start(bf16[96,1024]{1,0:T(8,128)(2,1)} %bitcast.7), channel_id=1, source_target_pairs={{0,8},{8,0},{16,24},{24,16},{1,9},{9,1},{17,25},{25,17},{2,10},{10... | collective-permute-start | bytes 589832 | tf_op jit(solution)/shard_map/ppermute | solution.py:385
  3.1 17.3 %collective-permute-start.11 = (bf16[96,1024]{1,0:T(8,128)(2,1)}, bf16[96,1024]{1,0:T(8,128)(2,1)S(1)}, u32[]{:S(2)}, u32[]{:S(2)}) collective-permute-start(bf16[96,1024]{1,0:T(8,128)(2,1)} %bitcast.8), channel_id=1, source_target_pairs={{0,16},{8,24},{16,0},{24,8},{1,17},{9,25},{17,1},{25,9},{2,18},{10... | collective-permute-start | bytes 589832 | tf_op jit(solution)/shard_map/ppermute | solution.py:385
  5.6 14.7 %collective-permute-start.12 = (bf16[96,1024]{1,0:T(8,128)(2,1)}, bf16[96,1024]{1,0:T(8,128)(2,1)S(1)}, u32[]{:S(2)}, u32[]{:S(2)}) collective-permute-start(bf16[96,1024]{1,0:T(8,128)(2,1)} %bitcast.9), channel_id=1, source_target_pairs={{0,24},{8,16},{16,8},{24,0},{1,25},{9,17},{17,9},{25,1},{2,26},{10... | collective-permute-start | bytes 589832 | tf_op jit(solution)/shard_map/ppermute | solution.py:385
  21.3 3.3 %copy-start.1 = (bf16[1,48,7168]{2,1,0:T(8,128)(2,1)S(1)}, bf16[1,48,7168]{2,1,0:T(8,128)(2,1)}, u32[]{:S(2)}) copy-start(bf16[1,48,7168]{2,1,0:T(8,128)(2,1)} %param.6) | copy-start | bytes 2064388
  24.5 2.7 %collective-permute-start.13 = (f32[128,2048]{1,0:T(8,128)S(1)}, f32[128,2048]{1,0:T(8,128)S(1)}, u32[]{:S(2)}, u32[]{:S(2)}) collective-permute-start(f32[128,2048]{1,0:T(8,128)S(1)} %get-tuple-element.18), channel_id=1, source_target_pairs={{0,1},{1,0},{2,3},{3,2},{4,5},{5,4},{6,7},{7,6},{8,9},{9,8},{10,11... | collective-permute-start | bytes 3145736 | tf_op jit(solution)/shard_map/ppermute | solution.py:35
  24.6 15.2 %collective-permute-start = (bf16[48,7168]{1,0:T(8,128)(2,1)S(1)}, bf16[48,7168]{1,0:T(8,128)(2,1)S(1)}, u32[]{:S(2)}, u32[]{:S(2)}) collective-permute-start(bf16[48,7168]{1,0:T(8,128)(2,1)S(1)} %bitcast.12), channel_id=1, source_target_pairs={{0,2},{1,5},{2,0},{3,7},{4,6},{5,1},{6,4},{7,3},{8,10},{9,13},{10,... | collective-permute-start | bytes 2064392 | tf_op jit(solution)/shard_map/ppermute | solution.py:41
  27.4 23.6 %collective-permute-start.14 = (f32[64,2048]{1,0:T(8,128)S(1)}, f32[64,2048]{1,0:T(8,128)S(1)}, u32[]{:S(2)}, u32[]{:S(2)}) collective-permute-start(f32[64,2048]{1,0:T(8,128)S(1)} %slice.17), channel_id=1, source_target_pairs={{0,2},{1,5},{2,0},{3,7},{4,6},{5,1},{6,4},{7,3},{8,10},{9,13},{10,... | collective-permute-start | bytes 1572872 | tf_op jit(solution)/shard_map/ppermute | solution.py:41
  29.0 26.1 %collective-permute-start.1 = (bf16[48,7168]{1,0:T(8,128)(2,1)S(1)}, bf16[48,7168]{1,0:T(8,128)(2,1)S(1)}, u32[]{:S(2)}, u32[]{:S(2)}) collective-permute-start(bf16[48,7168]{1,0:T(8,128)(2,1)S(1)} %bitcast.13), channel_id=1, source_target_pairs={{0,4},{1,3},{2,6},{3,1},{4,0},{5,7},{6,2},{7,5},{8,12},{9,11},{10,... | collective-permute-start | bytes 2064392 | tf_op jit(solution)/shard_map/ppermute | solution.py:41
  39.8 22.4 %copy-start.2 = (bf16[48,7168]{1,0:T(8,128)(2,1)}, bf16[48,7168]{1,0:T(8,128)(2,1)S(1)}, u32[]{:S(2)}) copy-start(bf16[48,7168]{1,0:T(8,128)(2,1)S(1)} %collective-permute-done.refs_1_) | copy-start | bytes 2064388
  39.8 15.7 %collective-permute-start.2 = (bf16[48,7168]{1,0:T(8,128)(2,1)S(1)}, bf16[48,7168]{1,0:T(8,128)(2,1)S(1)}, u32[]{:S(2)}, u32[]{:S(2)}) collective-permute-start(bf16[48,7168]{1,0:T(8,128)(2,1)S(1)} %collective-permute-done.refs_1_), channel_id=1, source_target_pairs={{0,4},{1,3},{2,6},{3,1},{4,0},{5,7},{6,2},{7,5},{8,12},{9,11},{10,... | collective-permute-start | bytes 2064392 | tf_op jit(solution)/shard_map/ppermute | solution.py:41
  51.9 7.2 %collective-permute-start.15 = (f32[32,2048]{1,0:T(8,128)}, f32[32,2048]{1,0:T(8,128)}, u32[]{:S(2)}, u32[]{:S(2)}) collective-permute-start(f32[32,2048]{1,0:T(8,128)} %slice.19), channel_id=1, source_target_pairs={{0,4},{1,3},{2,6},{3,1},{4,0},{5,7},{6,2},{7,5},{8,12},{9,11},{10,... | collective-permute-start | bytes 786440 | tf_op jit(solution)/shard_map/ppermute | solution.py:41
  54.4 7.7 %collective-permute-start.3 = (bf16[48,7168]{1,0:T(8,128)(2,1)S(1)}, bf16[48,7168]{1,0:T(8,128)(2,1)}, u32[]{:S(2)}, u32[]{:S(2)}) collective-permute-start(bf16[48,7168]{1,0:T(8,128)(2,1)S(1)} %bitcast.14), channel_id=1, source_target_pairs={{0,1},{1,0},{2,3},{3,2},{4,5},{5,4},{6,7},{7,6},{8,9},{9,8},{10,11... | collective-permute-start | bytes 2064392 | tf_op jit(solution)/shard_map/ppermute | solution.py:35
  54.5 7.6 %collective-permute-start.4 = (bf16[48,7168]{1,0:T(8,128)(2,1)S(1)}, bf16[48,7168]{1,0:T(8,128)(2,1)S(1)}, u32[]{:S(2)}, u32[]{:S(2)}) collective-permute-start(bf16[48,7168]{1,0:T(8,128)(2,1)S(1)} %collective-permute-done.refs_1_), channel_id=1, source_target_pairs={{0,1},{1,0},{2,3},{3,2},{4,5},{5,4},{6,7},{7,6},{8,9},{9,8},{10,11... | collective-permute-start | bytes 2064392 | tf_op jit(solution)/shard_map/ppermute | solution.py:35
  55.1 7.1 %copy-start.3 = (bf16[48,7168]{1,0:T(8,128)(2,1)}, bf16[48,7168]{1,0:T(8,128)(2,1)S(1)}, u32[]{:S(2)}) copy-start(bf16[48,7168]{1,0:T(8,128)(2,1)S(1)} %collective-permute-done.1.refs_2_) | copy-start | bytes 2064388
  55.1 7.1 %collective-permute-start.5 = (bf16[48,7168]{1,0:T(8,128)(2,1)S(1)}, bf16[48,7168]{1,0:T(8,128)(2,1)S(1)}, u32[]{:S(2)}, u32[]{:S(2)}) collective-permute-start(bf16[48,7168]{1,0:T(8,128)(2,1)S(1)} %collective-permute-done.1.refs_2_), channel_id=1, source_target_pairs={{0,1},{1,0},{2,3},{3,2},{4,5},{5,4},{6,7},{7,6},{8,9},{9,8},{10,11... | collective-permute-start | bytes 2064392 | tf_op jit(solution)/shard_map/ppermute | solution.py:35
  55.5 6.7 %copy-start.4 = (bf16[48,7168]{1,0:T(8,128)(2,1)}, bf16[48,7168]{1,0:T(8,128)(2,1)S(1)}, u32[]{:S(2)}) copy-start(bf16[48,7168]{1,0:T(8,128)(2,1)S(1)} %collective-permute-done.2.refs_3_) | copy-start | bytes 2064388
  55.5 6.7 %collective-permute-start.6 = (bf16[48,7168]{1,0:T(8,128)(2,1)S(1)}, bf16[48,7168]{1,0:T(8,128)(2,1)S(1)}, u32[]{:S(2)}, u32[]{:S(2)}) collective-permute-start(bf16[48,7168]{1,0:T(8,128)(2,1)S(1)} %collective-permute-done.2.refs_3_), channel_id=1, source_target_pairs={{0,1},{1,0},{2,3},{3,2},{4,5},{5,4},{6,7},{7,6},{8,9},{9,8},{10,11... | collective-permute-start | bytes 2064392 | tf_op jit(solution)/shard_map/ppermute | solution.py:35
  60.0 31.9 %collective-permute-start.16 = (bf16[32,2048]{1,0:T(8,128)(2,1)S(1)}, bf16[32,2048]{1,0:T(8,128)(2,1)S(1)}, u32[]{:S(2)}, u32[]{:S(2)}) collective-permute-start(bf16[32,2048]{1,0:T(8,128)(2,1)S(1)} %fusion.6), channel_id=1, source_target_pairs={{0,4},{1,3},{2,6},{3,1},{4,0},{5,7},{6,2},{7,5},{8,12},{9,11},{10,... | collective-permute-start | bytes 393224 | tf_op jit(solution)/shard_map/ppermute | solution.py:41
  78.8 14.7 %collective-permute-start.25 = (bf16[256,512]{1,0:T(8,128)(2,1)S(1)}, bf16[256,512]{1,0:T(8,128)(2,1)S(1)}, u32[]{:S(2)}, u32[]{:S(2)}) collective-permute-start(bf16[256,512]{1,0:T(8,128)(2,1)S(1)} %get-tuple-element.24), channel_id=1, source_target_pairs={{0,8},{24,16},{1,9},{25,17},{2,10},{26,18},{3,11},{27,19},{4,12},{... | collective-permute-start | bytes 786440 | tf_op jit(solution)/shard_map/ppermute | solution.py:412
  90.4 15.8 %collective-permute-start.19 = (bf16[256,1024]{1,0:T(8,128)(2,1)S(1)}, bf16[256,1024]{1,0:T(8,128)(2,1)S(1)}, u32[]{:S(2)}, u32[]{:S(2)}) collective-permute-start(bf16[256,1024]{1,0:T(8,128)(2,1)S(1)} %get-tuple-element.20), channel_id=1, source_target_pairs={{0,8},{24,16},{1,9},{25,17},{2,10},{26,18},{3,11},{27,19},{4,12},{... | collective-permute-start | bytes 1572872 | tf_op jit(solution)/shard_map/ppermute | solution.py:412
  92.0 14.0 %collective-permute-start.17 = (bf16[64,2048]{1,0:T(8,128)(2,1)S(1)}, bf16[64,2048]{1,0:T(8,128)(2,1)S(1)}, u32[]{:S(2)}, u32[]{:S(2)}) collective-permute-start(bf16[64,2048]{1,0:T(8,128)(2,1)S(1)} %pad_maximum_fusion.2), channel_id=1, source_target_pairs={{0,2},{1,5},{2,0},{3,7},{4,6},{5,1},{6,4},{7,3},{8,10},{9,13},{10,... | collective-permute-start | bytes 786440 | tf_op jit(solution)/shard_map/ppermute | solution.py:41
  93.6 12.5 %collective-permute-start.26 = (bf16[256,512]{1,0:T(8,128)(2,1)S(1)}, bf16[256,512]{1,0:T(8,128)(2,1)S(1)}, u32[]{:S(2)}, u32[]{:S(2)}) collective-permute-start(bf16[256,512]{1,0:T(8,128)(2,1)S(1)} %fusion.5), channel_id=1, source_target_pairs={{8,16},{16,8},{9,17},{17,9},{10,18},{18,10},{11,19},{19,11},{12,20... | collective-permute-start | bytes 786440 | tf_op jit(solution)/shard_map/ppermute | solution.py:412
  100.5 16.3 %collective-permute-start.7 = (bf16[256,1024]{1,0:T(8,128)(2,1)S(1)}, bf16[256,1024]{1,0:T(8,128)(2,1)S(1)}, u32[]{:S(2)}, u32[]{:S(2)}) collective-permute-start(bf16[256,1024]{1,0:T(8,128)(2,1)S(1)} %get-tuple-element.16), channel_id=1, source_target_pairs={{0,8},{24,16},{1,9},{25,17},{2,10},{26,18},{3,11},{27,19},{4,12},{... | collective-permute-start | bytes 1572872 | tf_op jit(solution)/shard_map/ppermute | solution.py:412
  104.6 21.2 %collective-permute-start.22 = (bf16[256,1024]{1,0:T(8,128)(2,1)S(1)}, bf16[256,1024]{1,0:T(8,128)(2,1)S(1)}, u32[]{:S(2)}, u32[]{:S(2)}) collective-permute-start(bf16[256,1024]{1,0:T(8,128)(2,1)S(1)} %get-tuple-element.22), channel_id=1, source_target_pairs={{0,8},{24,16},{1,9},{25,17},{2,10},{26,18},{3,11},{27,19},{4,12},{... | collective-permute-start | bytes 1572872 | tf_op jit(solution)/shard_map/ppermute | solution.py:412
  106.0 20.6 %collective-permute-start.18 = (bf16[128,2048]{1,0:T(8,128)(2,1)S(1)}, bf16[128,2048]{1,0:T(8,128)(2,1)S(1)}, u32[]{:S(2)}, u32[]{:S(2)}) collective-permute-start(bf16[128,2048]{1,0:T(8,128)(2,1)S(1)} %pad_maximum_fusion.1), channel_id=1, source_target_pairs={{0,1},{1,0},{2,3},{3,2},{4,5},{5,4},{6,7},{7,6},{8,9},{9,8},{10,11... | collective-permute-start | bytes 1572872 | tf_op jit(solution)/shard_map/ppermute | solution.py:35
  106.3 34.3 %collective-permute-start.20 = (bf16[256,1024]{1,0:T(8,128)(2,1)S(1)}, bf16[256,1024]{1,0:T(8,128)(2,1)S(1)}, u32[]{:S(2)}, u32[]{:S(2)}) collective-permute-start(bf16[256,1024]{1,0:T(8,128)(2,1)S(1)} %fusion.1), channel_id=1, source_target_pairs={{8,16},{16,8},{9,17},{17,9},{10,18},{18,10},{11,19},{19,11},{12,20... | collective-permute-start | bytes 1572872 | tf_op jit(solution)/shard_map/ppermute | solution.py:412
  117.0 25.2 %collective-permute-start.8 = (bf16[256,1024]{1,0:T(8,128)(2,1)S(1)}, bf16[256,1024]{1,0:T(8,128)(2,1)S(1)}, u32[]{:S(2)}, u32[]{:S(2)}) collective-permute-start(bf16[256,1024]{1,0:T(8,128)(2,1)S(1)} %fusion), channel_id=1, source_target_pairs={{8,16},{16,8},{9,17},{17,9},{10,18},{18,10},{11,19},{19,11},{12,20... | collective-permute-start | bytes 1572872 | tf_op jit(solution)/shard_map/ppermute | solution.py:412
  125.9 17.8 %collective-permute-start.23 = (bf16[256,1024]{1,0:T(8,128)(2,1)S(1)}, bf16[256,1024]{1,0:T(8,128)(2,1)S(1)}, u32[]{:S(2)}, u32[]{:S(2)}) collective-permute-start(bf16[256,1024]{1,0:T(8,128)(2,1)S(1)} %fusion.2), channel_id=1, source_target_pairs={{8,16},{16,8},{9,17},{17,9},{10,18},{18,10},{11,19},{19,11},{12,20... | collective-permute-start | bytes 1572872 | tf_op jit(solution)/shard_map/ppermute | solution.py:412
  129.9 24.8 %collective-permute-start.27 = (bf16[2,256,512]{2,1,0:T(8,128)(2,1)S(1)}, bf16[2,256,512]{2,1,0:T(8,128)(2,1)S(1)}, u32[]{:S(2)}, u32[]{:S(2)}) collective-permute-start(bf16[2,256,512]{2,1,0:T(8,128)(2,1)S(1)} %convert_element_type.88), channel_id=1, source_target_pairs={{0,8},{24,16},{1,9},{25,17},{2,10},{26,18},{3,11},{27,19},{4,12},{... | collective-permute-start | bytes 1572872 | tf_op jit(solution)/shard_map/ppermute | solution.py:427
  140.9 16.7 %collective-permute-start.21 = (bf16[256,1024]{1,0:T(8,128)(2,1)S(1)}, bf16[256,1024]{1,0:T(8,128)(2,1)S(1)}, u32[]{:S(2)}, u32[]{:S(2)}) collective-permute-start(bf16[256,1024]{1,0:T(8,128)(2,1)S(1)} %add_convert_fusion.1.kept_ref), channel_id=1, source_target_pairs={{8,0},{16,24},{9,1},{17,25},{10,2},{18,26},{11,3},{19,27},{12,4},{... | collective-permute-start | bytes 1572872 | tf_op jit(solution)/shard_map/ppermute | solution.py:432
  142.4 26.4 %collective-permute-start.9 = (bf16[256,1024]{1,0:T(8,128)(2,1)S(1)}, bf16[256,1024]{1,0:T(8,128)(2,1)S(1)}, u32[]{:S(2)}, u32[]{:S(2)}) collective-permute-start(bf16[256,1024]{1,0:T(8,128)(2,1)S(1)} %add_convert_fusion.2.kept_ref), channel_id=1, source_target_pairs={{8,0},{16,24},{9,1},{17,25},{10,2},{18,26},{11,3},{19,27},{12,4},{... | collective-permute-start | bytes 1572872 | tf_op jit(solution)/shard_map/ppermute | solution.py:432
  144.0 32.3 %collective-permute-start.24 = (bf16[256,1024]{1,0:T(8,128)(2,1)S(1)}, bf16[256,1024]{1,0:T(8,128)(2,1)S(1)}, u32[]{:S(2)}, u32[]{:S(2)}) collective-permute-start(bf16[256,1024]{1,0:T(8,128)(2,1)S(1)} %add_convert_fusion.kept_ref), channel_id=1, source_target_pairs={{8,0},{16,24},{9,1},{17,25},{10,2},{18,26},{11,3},{19,27},{12,4},{... | collective-permute-start | bytes 1572872 | tf_op jit(solution)/shard_map/ppermute | solution.py:432
  (4 other events, 3.7 us)
